TPU v7x, 512 devices: a whole 4x8x8 slice. The times are simulated.
512 devices in a mesh: utt: 8 (over x, core), tm: 64 (over y, z).
Axes of the slice: x: 4, y: 8, z: 8, core: 2. Of those that a mesh axis runs over, the one named last changes fastest.
Arguments:
- phone_ids: int32 [8, 4096], P('utt', 'tm'), may hold values from 0 to 255
- durations: int32 [8, 4096], P('utt'), may hold values from 1 to 16, 16384 in all within a row
- utt_lengths: int32 [8, 64], P('utt'), may hold values from 1 to 256, 4096 in all within a row
- utt_order: int32 [8, 64], P('utt'), may hold values from 0 to 63, each once within a row
- buckets: int32 [8, 64, 8], P('utt', 'tm'), may hold values from 0 to 7, each once within a row
- embed_table: bfloat16 [256, 384], replicated, may hold values from -6 to 6
- conv1_weight: bfloat16 [3456, 768], P(None, 'tm'), may hold values from -0.109375 to 0.109375
- conv2_weight: bfloat16 [384, 768], P(None, 'tm'), may hold values from -0.21875 to 0.21875
- norm_gain: float32 [384], replicated, may hold values from 0.1 to 1.9
- mel_weight: bfloat16 [384, 80], replicated, may hold values from -0.3125 to 0.3125
- pre_weight: bfloat16 [7, 80, 512], replicated, may hold values from -0.25 to 0.25
- up_weight: bfloat16 [512, 16, 256], P('tm'), may hold values from -0.1875 to 0.1875
Outputs:
- bucketed: bfloat16 [8, 64, 8, 256, 256], P('utt', 'tm')
All inputs are finite; a program needn't handle non-finite values.
Results may differ from a plain program's by a relative error of at most 0.0067.
Values may be sent and summed in bfloat16 or wider, within the bound.
A program may use at most 64 MiB of HBM per device.

v0:
```python
import jax
import jax.numpy as jnp
from jax import lax
from jax.sharding import PartitionSpec as P

F_DEV = 256


EPS = 1e-05


def padded(cells, sides, width):
    for axis, dim in sides:
        count = lax.axis_size(axis)
        ends = count - 1
        head = lax.slice_in_dim(cells, 0, width, axis=dim)
        tail = lax.slice_in_dim(cells, cells.shape[dim] - width, cells.shape[dim], axis=dim)
        cells = jnp.concatenate(
            [
                lax.ppermute(tail, axis, [(i, (i + 1) % count) for i in range(ends)]),
                cells,
                lax.ppermute(head, axis, [((i + 1) % count, i) for i in range(ends)]),
            ],
            axis=dim,
        )
    return cells


def utterance_of(indices, bounds):
    return jnp.sum((bounds[None, :] <= indices[:, None]).astype(jnp.int32), axis=1)


def frame_layout(lasting, lengths, ordering):
    phone_total = lasting.shape[0]
    utt_count = lengths.shape[0]
    phone_index = jnp.arange(phone_total, dtype=jnp.int32)
    bounds = jnp.cumsum(lengths)
    utt_first = bounds - lengths
    owners = utterance_of(phone_index, bounds)
    inclusive = jnp.cumsum(lasting)
    exclusive = inclusive - lasting
    first_frame = jnp.take(exclusive, utt_first)
    utt_frames = jnp.take(inclusive, bounds - 1) - first_frame
    slots = jnp.arange(utt_count, dtype=jnp.int32)
    places = jnp.sum(jnp.where(ordering[None, :] == slots[:, None], slots[None, :], 0), axis=1)
    offsets = jnp.sum(jnp.where(places[None, :] < places[:, None], utt_frames[None, :], 0), axis=1)
    starting = jnp.take(offsets, owners) + exclusive - jnp.take(first_frame, owners)
    return (starting, owners, bounds)


def masked_unfold(row_block, labels, offset, amount, width_taps, reach):
    center = labels[offset : offset + amount]
    columns = []
    for tap in range(width_taps):
        anchor = offset - reach + tap
        keep = (labels[anchor : anchor + amount] == center)[:, None]
        columns.append(
            jnp.where(keep, row_block[anchor : anchor + amount], jnp.zeros((), row_block.dtype))
        )
    return jnp.concatenate(columns, axis=1)


def shards(
    phone_ids,
    durations,
    utt_lengths,
    utt_order,
    buckets,
    embed_table,
    conv1_weight,
    conv2_weight,
    norm_gain,
    mel_weight,
    pre_weight,
    up_weight,
):
    phone_count = phone_ids.shape[1]
    device = lax.axis_index("tm")
    lasting = durations[0]
    starting, owners, bounds = frame_layout(lasting, utt_lengths[0], utt_order[0])
    ending = starting + lasting
    nearby = device * phone_count + jnp.arange(-4, phone_count + 4, dtype=jnp.int32)
    phone_labels = jnp.where(nearby < 0, -1, utterance_of(nearby, bounds))
    symbols = embed_table.shape[0]
    choose = (phone_ids[0][:, None] == jnp.arange(symbols, dtype=jnp.int32)[None, :]).astype(
        jnp.bfloat16
    )
    embedded = jnp.dot(choose, embed_table, preferred_element_type=jnp.float32).astype(jnp.bfloat16)
    widened = padded(embedded, (("tm", 0),), 4)
    unfolded = masked_unfold(widened, phone_labels, 4, phone_count, 9, 4)
    inward = lax.all_gather(conv1_weight, "tm", axis=1, tiled=True)
    outward = lax.all_gather(conv2_weight, "tm", axis=1, tiled=True)
    filters = jnp.maximum(
        jnp.dot(unfolded, inward, preferred_element_type=jnp.float32), 0.0
    ).astype(jnp.bfloat16)
    conv_out = lax.dot_general(
        filters, outward, (((1,), (1,)), ((), ())), preferred_element_type=jnp.float32
    )
    resid = embedded.astype(jnp.float32) + conv_out
    center = jnp.mean(resid, axis=1, keepdims=True)
    spread = jnp.mean((resid - center) ** 2, axis=1, keepdims=True)
    decoded = ((resid - center) * lax.rsqrt(spread + EPS) * norm_gain[None, :]).astype(jnp.bfloat16)
    span = F_DEV + 8
    frames = device * F_DEV - 4 + jnp.arange(span, dtype=jnp.int32)
    mel_width = mel_weight.shape[1]
    portion = lax.all_gather(decoded, "tm", axis=0, tiled=True)
    hit = (frames[:, None] >= starting[None, :]) & (frames[:, None] < ending[None, :])
    sums = jnp.dot(hit.astype(jnp.bfloat16), portion, preferred_element_type=jnp.float32)
    marks = jnp.sum(jnp.where(hit, owners[None, :] + 1, 0), axis=1)
    sums, marks = (sums, marks)
    mel_frames = jnp.dot(
        sums.astype(jnp.bfloat16), mel_weight, preferred_element_type=jnp.float32
    ).astype(jnp.bfloat16)
    frame_labels = marks - 1
    channels = pre_weight.shape[2]
    pre_flat = pre_weight.reshape(7 * mel_width, channels)
    columns = masked_unfold(mel_frames, frame_labels, 4, F_DEV, 7, 3)
    summed = jnp.dot(columns, pre_flat, preferred_element_type=jnp.float32)
    act_wide = padded(
        jnp.where(summed >= 0, summed, 0.1 * summed).astype(jnp.bfloat16), (("tm", 0),), 1
    )
    center_labels = frame_labels[4 : 4 + F_DEV]
    same_prev = (frame_labels[3 : 3 + F_DEV] == center_labels)[:, None]
    same_next = (frame_labels[5 : 5 + F_DEV] == center_labels)[:, None]
    act_mid = act_wide[1 : F_DEV + 1]
    act_prev = jnp.where(same_prev, act_wide[0:F_DEV], jnp.zeros((), jnp.bfloat16))
    act_next = jnp.where(same_next, act_wide[2 : F_DEV + 2], jnp.zeros((), jnp.bfloat16))
    out_width = up_weight.shape[2]
    groups = lax.axis_size("utt")
    placing = buckets[0, 0]
    selector = (placing[None, :] == jnp.arange(groups, dtype=jnp.int32)[:, None]).astype(
        jnp.bfloat16
    )
    portion = lax.all_gather(up_weight, "tm", axis=0, tiled=True)
    amount = portion.shape[0]
    weights = portion.reshape(amount, 16 * out_width)
    middle = jnp.dot(
        act_mid, weights[:, 4 * out_width : 12 * out_width], preferred_element_type=jnp.float32
    )
    before = jnp.dot(act_prev, weights[:, 12 * out_width :], preferred_element_type=jnp.float32)
    after = jnp.dot(act_next, weights[:, : 4 * out_width], preferred_element_type=jnp.float32)
    upsampled = middle + jnp.concatenate([before, after], axis=1)
    segments = upsampled.astype(jnp.bfloat16).reshape(groups, -1, out_width)
    outgoing = jnp.einsum(
        "bj,jsc->bsc", selector, segments, preferred_element_type=jnp.float32
    ).astype(jnp.bfloat16)
    arrived = lax.all_to_all(outgoing, "utt", split_axis=0, concat_axis=0, tiled=True)
    return arrived.reshape(1, 1, groups, -1, out_width)


def solution(mesh):
    placed = (
        P("utt", "tm"),
        P("utt", None),
        P("utt", None),
        P("utt", None),
        P("utt", "tm", None),
        P(),
        P(None, "tm"),
        P(None, "tm"),
        P(),
        P(),
        P(),
        P("tm", None, None),
    )
    return jax.shard_map(
        shards,
        mesh=mesh,
        in_specs=placed,
        out_specs=P("utt", "tm", None, None, None),
        check_vma=False,
    )
```

profile of v0, /device:TPU:1, one launch (start us, length us, event | category | flops | bytes accessed | tf_op | source)
XLA Modules:
  0.0 333.1 jit_solution(16332967862284316481)
XLA Ops:
  6.5 0.7 all-gather.10.cloned.1.call-update
  7.3 1.1 convolution_convert_fusion.1
  8.5 4.8 %collective-permute-start = (bf16[4,384]{1,0:T(4,128)(2,1)S(1)}, bf16[4,384]{1,0:T(4,128)(2,1)S(1)}, u32[]{:S(2)}, u32[]{:S(2)}) collective-permute-start(bf16[4,384]{1,0:T(4,128)(2,1)S(1)} %get-tuple-element.16), channel_id=1, source_target_pairs={{0,1},{1,2},{2,3},{3,4},{4,5},{5,6},{6,7},{7,8},{8,9},{9,10},{10,1... | collective-permute-start | bytes 9224 | tf_op jit(solution)/shard_map/ppermute | solution.py:20
  13.3 1.3 collective-permute-start.1
  14.6 0.7 copy.22
  15.3 0.1 reduce-window.21
  15.4 0.1 reduce
  15.6 0.1 convert_reduce_fusion.1
  15.7 0.1 slice_compare_fusion.6
  15.7 48.4 %all-gather.1 = bf16[64,12,384]{2,1,0:T(8,128)(2,1)S(1)} all-gather(bf16[1,12,384]{2,1,0:T(8,128)(2,1)} %bitcast.173), channel_id=1, replica_groups=mesh['utt'=8,'tm'=64] {'tm'}, dimensions={0}, use_global_device_ids=true | all-gather | bytes 599040 | tf_op jit(solution)/shard_map/all_gather | solution.py:92
  64.1 0.1 reshape.281
  64.3 0.1 fusion.43
  64.3 0.1 fusion.46
  64.4 0.1 fusion.40
  64.5 0.1 fusion.50
  64.6 0.1 fusion.34
  64.7 0.1 fusion.37
  64.8 0.1 fusion.31
  64.9 0.1 fusion.48
  65.0 44.1 %all-gather.10.cloned.1.call-done = bf16[64,12,3456]{2,1,0:T(8,128)(2,1)} async-done(((bf16[1,12,3456]{2,1,0:T(8,128)(2,1)}), bf16[64,12,3456]{2,1,0:T(8,128)(2,1)}) %all-gather.10.cloned.1.call-update) | async-done | bytes 5308432 | tf_op jit(solution)/shard_map/all_gather | solution.py:91
  109.1 9.2 %reshape.279 = bf16[768,3456]{1,0:T(8,128)(2,1)} reshape(bf16[64,12,3456]{2,1,0:T(8,128)(2,1)} %all-gather.10.cloned.1.call-done) | data formatting | bytes 10616832
  118.4 4.6 %fusion.79 = (f32[64]{0:T(128)S(1)}, f32[64,384]{1,0:T(8,128)S(1)}) fusion(bf16[768,384]{1,0:T(8,128)(2,1)S(1)} %reshape.281, bf16[64,3456]{1,0:T(8,128)(2,1)S(1)} %fusion.48, bf16[768,3456]{1,0:T(8,128)(2,1)} %reshape.279, bf16[64,384]{1,0:T(8,128)(2,1)S(1)} %convolution_convert_fusion.1), kind=kOutput, calls=%fused_computation.146 | convolution fusion | flops 377659328 | bytes 6488320 | tf_op jit(solution)/shard_map/dot_general | solution.py:96
  122.9 0.2 multiply_reduce_fusion
  123.1 0.7 multiply_convert_fusion
  123.9 0.7 all-gather.8.cloned.1.call-update
  124.6 0.3 reduce-window.19
  125.1 0.1 slice_reduce_fusion
  125.3 0.8 gather_fusion.1
  126.0 0.8 gather_fusion
  126.8 0.1 select_reduce_fusion.2
  127.0 0.2 select_reduce_fusion.1
  127.1 0.7 fusion.74
  127.8 0.7 fusion.78
  128.5 0.7 fusion.73
  129.2 0.7 fusion.72
  129.9 0.7 fusion.71
  130.6 0.7 fusion.76
  131.4 0.7 fusion.75
  132.1 0.7 fusion.77
  132.8 0.2 convert_reduce_fusion
  133.0 80.0 %fusion.67 = (s32[4096]{0:T(1024)S(1)}, s32[4096]{0:T(1024)S(1)}) fusion(s32[4096]{0:T(1024)S(1)} %bitcast.171, s32[]{:T(128)} %bitcast.135, s32[]{:T(128)} %bitcast.134, s32[]{:T(128)} %bitcast.133, s32[]{:T(128)} %bitcast.132, s32[]{:T(128)} %bitcast.131, s32[]{:T(128)} %bitcast.130, s32[]{:T(128)} %bitcast.129, s32[]{:T(128)} %bitcast.128, s32[]{:T(128)} %bitcast.127, ...), kind=kLoop, calls=%fused_computation.134 | loop fusion | flops 819200 | bytes 82432 | tf_op jit(solution)/shard_map/add | solution.py:81
  213.1 0.9 select_reduce_fusion
  214.1 3.4 %fusion.11 = bf16[264,80]{0,1:T(8,128)(2,1)S(1)} fusion(bf16[384,80]{0,1:T(8,128)(2,1)S(1)} %copy-done.5, bf16[4096,384]{1,0:T(8,128)(2,1)} %all-gather.6.cloned.1.call-done, s32[4096]{0:T(1024)S(1)} %get-tuple-element.6, s32[4096]{0:T(1024)S(1)} %get-tuple-element.8, s32[264]{0:T(512)S(1)} %iota_add_fusion), kind=kOutput, calls=%fused_computation.19 | convolution fusion | flops 850058880 | bytes 3283232 | tf_op jit(solution)/shard_map/dot_general | solution.py:111
  217.5 0.1 fusion.56
  217.6 0.1 fusion.55
  217.7 0.1 fusion.54
  217.8 0.1 slice_dynamic-update-slice_fusion
  217.9 0.1 fusion.53
  218.0 0.1 fusion.52
  218.0 0.1 fusion.51
  218.1 0.4 fusion.17
  218.6 1.3 collective-permute-start.2
  219.8 69.4 %all-gather.8.cloned.1.call-done = bf16[512,16,256]{2,1,0:T(8,128)(2,1)} async-done(((bf16[8,16,256]{2,1,0:T(8,128)(2,1)}), bf16[512,16,256]{2,1,0:T(8,128)(2,1)}) %all-gather.8.cloned.1.call-update) | async-done | bytes 4194320 | tf_op jit(solution)/shard_map/all_gather | solution.py:134
  289.2 4.4 %copy.25 = bf16[64,8,16,256]{3,1,2,0:T(8,128)(2,1)S(1)} copy(bf16[64,8,16,256]{3,2,1,0:T(8,128)(2,1)} %bitcast.164) | data formatting | bytes 8388608
  293.6 1.5 collective-permute-start.3
  295.1 0.5 fusion.14
  295.6 2.4 collective-permute-done.3
  298.0 0.5 fusion.12
  298.5 0.7 fusion.1
  299.2 0.5 reshape.114
  299.7 0.7 convolution_convert_fusion
  300.4 0.2 copy.24
  300.7 25.0 %all_to_all.5 = bf16[8,256,256]{2,1,0:T(8,128)(2,1)S(1)} all-to-all(bf16[8,256,256]{2,1,0:T(8,128)(2,1)S(1)} %copy.24), channel_id=1, replica_groups=mesh['utt'=8,'tm'=64] {'utt'}, dimensions={0} | all-to-all | bytes 2097152 | tf_op jit(solution)/shard_map/all_to_all | solution.py:147
  325.6 1.0 copy.43
  (39 shorter events, 0.5 us)
Async XLA Ops:
  6.5 211.6 %copy-start = (bf16[7,80,512]{2,1,0:T(8,128)(2,1)S(1)}, bf16[7,80,512]{2,1,0:T(8,128)(2,1)}, u32[]{:S(2)}) copy-start(bf16[7,80,512]{2,1,0:T(8,128)(2,1)} %param.26) | copy-start | bytes 1720324
  6.5 102.6 %all-gather.10.cloned.1.call-start = ((), (), s32[]{:S(2)}) async-start(), calls=%async_computation.3 | async-start | bytes 7188480 | tf_op jit(solution)/shard_map/all_gather | solution.py:91
  7.3 206.8 %all-gather.6.cloned.1.call-start = ((), (), s32[]{:S(2)}) async-start(), calls=%async_computation.1 | async-start | bytes 3194880 | tf_op jit(solution)/shard_map/all_gather | solution.py:106
  8.5 55.8 %collective-permute-start = (bf16[4,384]{1,0:T(4,128)(2,1)S(1)}, bf16[4,384]{1,0:T(4,128)(2,1)S(1)}, u32[]{:S(2)}, u32[]{:S(2)}) collective-permute-start(bf16[4,384]{1,0:T(4,128)(2,1)S(1)} %get-tuple-element.16), channel_id=1, source_target_pairs={{0,1},{1,2},{2,3},{3,4},{4,5},{5,6},{6,7},{7,8},{8,9},{9,10},{10,1... | collective-permute-start | bytes 9224 | tf_op jit(solution)/shard_map/ppermute | solution.py:20
  13.3 51.3 %collective-permute-start.1 = (bf16[4,384]{1,0:T(4,128)(2,1)S(1)}, bf16[4,384]{1,0:T(4,128)(2,1)S(1)}, u32[]{:S(2)}, u32[]{:S(2)}) collective-permute-start(bf16[4,384]{1,0:T(4,128)(2,1)S(1)} %get-tuple-element.15), channel_id=1, source_target_pairs={{1,0},{2,1},{3,2},{4,3},{5,4},{6,5},{7,6},{8,7},{9,8},{10,9},{11,1... | collective-permute-start | bytes 9224 | tf_op jit(solution)/shard_map/ppermute | solution.py:22
  118.3 4.8 %copy-start.2 = (f32[384]{0:T(512)S(1)}, f32[384]{0:T(512)}, u32[]{:S(2)}) copy-start(f32[384]{0:T(512)} %param.24) | copy-start | bytes 4612
  118.3 6.3 %copy-start.1 = (s32[1,4096]{1,0:T(1,128)S(1)}, s32[1,4096]{1,0:T(1,128)}, u32[]{:S(2)}) copy-start(s32[1,4096]{1,0:T(1,128)} %param.17) | copy-start | bytes 49156
  118.3 6.7 %copy-start.3 = (s32[1,64]{1,0:T(1,128)S(1)}, s32[1,64]{1,0:T(1,128)}, u32[]{:S(2)}) copy-start(s32[1,64]{1,0:T(1,128)} %param.18) | copy-start | bytes 772
  118.3 8.5 %copy-start.6 = (s32[1,64]{1,0:T(1,128)S(1)}, s32[1,64]{1,0:T(1,128)}, u32[]{:S(2)}) copy-start(s32[1,64]{1,0:T(1,128)} %param.19) | copy-start | bytes 772
  118.3 95.8 %copy-start.5 = (bf16[384,80]{0,1:T(8,128)(2,1)S(1)}, bf16[384,80]{0,1:T(8,128)(2,1)}, u32[]{:S(2)}) copy-start(bf16[384,80]{0,1:T(8,128)(2,1)} %param.25) | copy-start | bytes 184324
  123.9 165.4 %all-gather.8.cloned.1.call-start = ((), (), s32[]{:S(2)}) async-start(), calls=%async_computation.2 | async-start | bytes 4259840 | tf_op jit(solution)/shard_map/all_gather | solution.py:134
  218.6 76.6 %collective-permute-start.2 = (bf16[1,512]{1,0:T(2,128)(2,1)S(1)}, bf16[1,512]{1,0:T(2,128)(2,1)S(1)}, u32[]{:S(2)}, u32[]{:S(2)}) collective-permute-start(bf16[1,512]{1,0:T(2,128)(2,1)S(1)} %get-tuple-element.13), channel_id=1, source_target_pairs={{0,1},{1,2},{2,3},{3,4},{4,5},{5,6},{6,7},{7,8},{8,9},{9,10},{10,1... | collective-permute-start | bytes 3080 | tf_op jit(solution)/shard_map/ppermute | solution.py:20
  293.6 4.3 %collective-permute-start.3 = (bf16[1,512]{1,0:T(2,128)(2,1)S(1)}, bf16[1,512]{1,0:T(2,128)(2,1)S(1)}, u32[]{:S(2)}, u32[]{:S(2)}) collective-permute-start(bf16[1,512]{1,0:T(2,128)(2,1)S(1)} %get-tuple-element.14), channel_id=1, source_target_pairs={{1,0},{2,1},{3,2},{4,3},{5,4},{6,5},{7,6},{8,7},{9,8},{10,9},{11,1... | collective-permute-start | bytes 3080 | tf_op jit(solution)/shard_map/ppermute | solution.py:22
  298.5 1.3 copy-start.4
Sparse Core Ops, SparseCore 0:
  10.4 98.6 all-gather.9
  124.0 79.0 all-gather.5
  206.1 83.0 all-gather.7
where the time goes:
time: 335 us; the launch traced here: 333 us
  waiting for transfers between devices  117 us (35%)
  other arithmetic  84.5 us (25%)
  blocking collectives  73.4 us (22%)
  local copies, waits for them, and re-layouts  23.8 us (7%)
  between operations  13.5 us (4%)
  matrix products  11.9 us (4%)
  starting transfers between devices  8.95 us (3%)
    add x1, other arithmetic, shards(): ending = starting + lasting  80 us
    all_gather x1, waiting for transfers between devices, shards(): portion = lax.all_gather(up_weight, 'tm', axis=0, tiled=True)  69.4 us
    all_gather x1, blocking collectives, shards(): outward = lax.all_gather(conv2_weight, 'tm', axis=1, tiled=True)  48.4 us
    all_gather x1, waiting for transfers between devices, shards(): inward = lax.all_gather(conv1_weight, 'tm', axis=1, tiled=True)  44.1 us
    all_to_all x1, blocking collectives, shards(): lax.all_to_all(outgoing, 'utt', split_axis=0, concat_axis=0, tiled=True)  25 us
    unnamed x20, local copies, waits for them, and re-layouts  14.8 us
  transfers between devices with their start and end apart: 7, of which 3 were waited for; matrix products, arithmetic and copies ran while one was open for 31% of the time, Pallas kernels for 0%

commit v1 on v0

v1 whole, which is shorter than its diff:
```python
import functools

import jax
import jax.numpy as jnp
from jax import lax
from jax.experimental import pallas as pl
from jax.experimental.pallas import tpu as pltpu
from jax.sharding import PartitionSpec as P

F_DEV = 256
SIDE = 8
WIDE = 128
REACH = 4
EPS = 1e-05
MESH = pl.DeviceIdType.MESH
BF = jnp.bfloat16


def gather_kernel(count, share, *refs):
    blocks = refs[:count]
    outs = refs[count : 2 * count]
    local_sem, first_send, first_recv, ring_send, ring_recv, pair_send, pair_recv = refs[2 * count :]
    utt = lax.axis_index("utt")
    tm = lax.axis_index("tm")
    core = lax.rem(utt, 2)
    pair = utt + 1 - 2 * core
    y = lax.div(tm, SIDE)
    z = lax.rem(tm, SIDE)
    first = y + core * (z - y)
    second = z + core * (y - z)
    half = core if share else 0

    def place(a, b):
        return a * SIDE + b + core * ((b - a) * SIDE + (a - b))

    barrier = pltpu.get_barrier_semaphore()

    def greet(step, carry):
        pl.semaphore_signal(
            barrier, inc=1,
            device_id=(utt, place(lax.rem(first + step, SIDE), second)), device_id_type=MESH,
        )
        return carry

    lax.fori_loop(1, SIDE, greet, 0)
    up = lax.rem(second + 1, SIDE)
    down = lax.rem(second + SIDE - 1, SIDE)
    for side in (up, down):
        pl.semaphore_signal(barrier, inc=1, device_id=(utt, place(first, side)), device_id_type=MESH)
    if share:
        pl.semaphore_signal(barrier, inc=1, device_id=(pair, tm), device_id_type=MESH)
    pl.semaphore_wait(barrier, SIDE + 1 + (1 if share else 0))

    own = [
        pltpu.make_async_copy(blocks[i], outs[i].at[half, second, first], local_sem.at[i])
        for i in range(count)
    ]
    for copy in own:
        copy.start()

    def first_copy(i, step):
        return pltpu.make_async_remote_copy(
            src_ref=blocks[i],
            dst_ref=outs[i].at[half, second, first],
            send_sem=first_send.at[i, step],
            recv_sem=first_recv.at[i, step],
            device_id=(utt, place(lax.rem(first + step, SIDE), second)),
            device_id_type=MESH,
        )

    for i in range(count):
        for step in range(1, SIDE):
            first_copy(i, step).start()
    for copy in own:
        copy.wait()
    for i in range(count):
        for step in range(1, SIDE):
            first_copy(i, step).wait_recv()

    def ring_copy(i, way, step):
        slot = lax.rem(second - step + SIDE, SIDE) if way == 0 else lax.rem(second + step, SIDE)
        row = outs[i].at[half, slot]
        return pltpu.make_async_remote_copy(
            src_ref=row,
            dst_ref=row,
            send_sem=ring_send.at[i, way, step],
            recv_sem=ring_recv.at[i, way, step],
            device_id=(utt, place(first, up if way == 0 else down)),
            device_id_type=MESH,
        )

    def pair_copy(i, slot, number):
        row = outs[i].at[half, slot]
        return pltpu.make_async_remote_copy(
            src_ref=row,
            dst_ref=row,
            send_sem=pair_send.at[i, number],
            recv_sem=pair_recv.at[i, number],
            device_id=(pair, tm),
            device_id_type=MESH,
        )

    pairs = []

    def hand_over(i, slot, number):
        if share:
            copy = pair_copy(i, slot, number)
            copy.start()
            pairs.append(copy)

    ways = ((0, SIDE // 2), (1, SIDE // 2 - 1))
    for i in range(count):
        for way, _ in ways:
            ring_copy(i, way, 0).start()
        hand_over(i, second, 0)
    for step in range(SIDE // 2):
        for i in range(count):
            for way, steps in ways:
                if step < steps:
                    ring_copy(i, way, step).wait_recv()
                    if step + 1 < steps:
                        ring_copy(i, way, step + 1).start()
                    if way == 0:
                        slot = lax.rem(second - step - 1 + SIDE, SIDE)
                    else:
                        slot = lax.rem(second + step + 1, SIDE)
                    hand_over(i, slot, 1 + 2 * step + way)
    for copy in pairs:
        copy.wait_recv()
    for i in range(count):
        for step in range(1, SIDE):
            first_copy(i, step).wait_send()
        for way, steps in ways:
            for step in range(steps):
                ring_copy(i, way, step).wait_send()
    for copy in pairs:
        copy.wait_send()


def gather_blocks(blocks, share, number):
    count = len(blocks)
    halves = 2 if share else 1
    return pl.pallas_call(
        functools.partial(gather_kernel, count, share),
        out_shape=[
            jax.ShapeDtypeStruct((halves, SIDE, SIDE) + block.shape, block.dtype) for block in blocks
        ],
        in_specs=[pl.BlockSpec(memory_space=pl.ANY)] * count,
        out_specs=[pl.BlockSpec(memory_space=pl.ANY)] * count,
        scratch_shapes=[
            pltpu.SemaphoreType.DMA((count,)),
            pltpu.SemaphoreType.DMA((count, SIDE)),
            pltpu.SemaphoreType.DMA((count, SIDE)),
            pltpu.SemaphoreType.DMA((count, 2, SIDE // 2)),
            pltpu.SemaphoreType.DMA((count, 2, SIDE // 2)),
            pltpu.SemaphoreType.DMA((count, SIDE)),
            pltpu.SemaphoreType.DMA((count, SIDE)),
        ],
        compiler_params=pltpu.CompilerParams(collective_id=number, has_side_effects=True),
        name=f"gather{number}",
    )(*blocks)


def utterance_of(indices, bounds):
    return jnp.sum((bounds[None, :] <= indices[:, None]).astype(jnp.int32), axis=1)


def frame_layout(lasting, lengths, ordering):
    phone_total = lasting.shape[0]
    utt_count = lengths.shape[0]
    phone_index = jnp.arange(phone_total, dtype=jnp.int32)
    bounds = jnp.cumsum(lengths)
    utt_first = bounds - lengths
    inclusive = jnp.cumsum(lasting)
    exclusive = inclusive - lasting
    first_frame = jnp.take(exclusive, utt_first)
    utt_frames = jnp.take(inclusive, bounds - 1) - first_frame
    slots = jnp.arange(utt_count, dtype=jnp.int32)
    places = jnp.sum(jnp.where(ordering[None, :] == slots[:, None], slots[None, :], 0), axis=1)
    offsets = jnp.sum(jnp.where(places[None, :] < places[:, None], utt_frames[None, :], 0), axis=1)
    moved = offsets - first_frame
    member = (bounds[None, :] > phone_index[:, None]) & (utt_first[None, :] <= phone_index[:, None])
    starting = exclusive + jnp.sum(jnp.where(member, moved[None, :], 0), axis=1)
    return (starting, bounds)


def shards(
    phone_ids,
    durations,
    utt_lengths,
    utt_order,
    buckets,
    embed_table,
    conv1_weight,
    conv2_weight,
    norm_gain,
    mel_weight,
    pre_weight,
    up_weight,
):
    phone_count = phone_ids.shape[1]
    width = embed_table.shape[1]
    device = lax.axis_index("tm")
    core = lax.rem(lax.axis_index("utt"), 2)
    ends = lax.axis_size("tm") - 1

    filters_here = conv1_weight.shape[1]
    part = filters_here // 2
    pad = ((0, 0), (0, 8 - part), (0, 0))
    inward = jnp.pad(conv1_weight.T.reshape(2, part, -1), pad)
    outward = jnp.pad(conv2_weight.T.reshape(2, part, -1), pad)
    rising = jnp.transpose(up_weight, (1, 0, 2)).reshape(2, 8, up_weight.shape[0], -1)
    pick = lambda both: jnp.where(core == 0, both[0], both[1])
    inward, outward, rising = gather_blocks([pick(inward), pick(outward), pick(rising)], True, 1)
    rows = 2 * SIDE * SIDE * 8
    inward = inward.reshape(rows, -1)
    outward = outward.reshape(rows, -1)

    starting, bounds = frame_layout(durations[0], utt_lengths[0], utt_order[0])
    ending = starting + durations[0]
    nearby = device * phone_count + jnp.arange(-4, phone_count + 4, dtype=jnp.int32)
    phone_labels = jnp.where(nearby < 0, -1, utterance_of(nearby, bounds))
    head = lax.ppermute(phone_ids[0, :4], "tm", [(i + 1, i) for i in range(ends)])
    tail = lax.ppermute(phone_ids[0, -4:], "tm", [(i, i + 1) for i in range(ends)])
    ids = jnp.concatenate([tail, phone_ids[0], head])
    symbols = embed_table.shape[0]
    choose = (ids[:, None] == jnp.arange(symbols, dtype=jnp.int32)[None, :]).astype(BF)
    widened = jnp.dot(choose, embed_table, preferred_element_type=jnp.float32).astype(BF)
    center = phone_labels[4 : 4 + phone_count]
    columns = []
    for tap in range(9):
        keep = (phone_labels[tap : tap + phone_count] == center)[:, None]
        columns.append(jnp.where(keep, widened[tap : tap + phone_count], jnp.zeros((), BF)))
    unfolded = jnp.concatenate(columns, axis=1)
    filters = jnp.maximum(
        lax.dot_general(
            unfolded, inward, (((1,), (1,)), ((), ())), preferred_element_type=jnp.float32
        ),
        0.0,
    ).astype(BF)
    conv_out = jnp.dot(filters, outward, preferred_element_type=jnp.float32)
    resid = widened[4 : 4 + phone_count].astype(jnp.float32) + conv_out
    middle = jnp.mean(resid, axis=1, keepdims=True)
    spread = jnp.mean((resid - middle) ** 2, axis=1, keepdims=True)
    decoded = ((resid - middle) * lax.rsqrt(spread + EPS) * norm_gain[None, :]).astype(BF)
    mel_width = mel_weight.shape[1]
    mel_ph = jnp.dot(decoded, mel_weight, preferred_element_type=jnp.float32).astype(BF)
    lane = lax.broadcasted_iota(jnp.int32, (phone_count, WIDE), 1)
    told = jnp.where(lane == mel_width, (center + 1).astype(BF)[:, None], jnp.zeros((), BF))
    mel_block = jnp.pad(mel_ph, ((0, 0), (0, WIDE - mel_width))) + told
    (portion,) = gather_blocks([mel_block], False, 2)
    portion = portion.reshape(-1, WIDE)

    def arranged(values):
        cells = values.reshape(SIDE, SIDE, phone_count)
        return jnp.where(core == 0, jnp.transpose(cells, (1, 0, 2)), cells).reshape(-1)

    groups = lax.axis_size("utt")
    piece = F_DEV // groups
    span = piece + 2 * REACH
    slots = jnp.arange(groups, dtype=jnp.int32)
    source = jnp.sum(
        jnp.where(buckets[0, 0][None, :] == slots[:, None], slots[None, :], 0), axis=1
    )
    frames = (
        device * F_DEV + source[:, None] * piece - REACH
        + jnp.arange(span, dtype=jnp.int32)[None, :]
    ).reshape(-1)
    hit = (frames[:, None] >= arranged(starting)[None, :]) & (
        frames[:, None] < arranged(ending)[None, :]
    )
    windows = jnp.dot(hit.astype(BF), portion, preferred_element_type=jnp.float32).astype(BF)
    arrived = lax.all_to_all(
        windows.reshape(groups, span, WIDE), "utt", split_axis=0, concat_axis=0, tiled=True
    )

    labels = arrived[:, :, mel_width]
    channels = pre_weight.shape[2]
    pre_flat = jnp.pad(pre_weight, ((0, 0), (0, WIDE - mel_width), (0, 0))).reshape(-1, channels)
    inner = piece + 2
    mine = labels[:, 3 : 3 + inner]
    columns = []
    for tap in range(7):
        keep = (labels[:, tap : tap + inner] == mine)[:, :, None]
        columns.append(jnp.where(keep, arrived[:, tap : tap + inner], jnp.zeros((), BF)))
    unfolded = jnp.concatenate(columns, axis=2).reshape(groups * inner, -1)
    summed = jnp.dot(unfolded, pre_flat, preferred_element_type=jnp.float32)
    act = jnp.where(summed >= 0, summed, 0.1 * summed).astype(BF).reshape(groups, inner, channels)
    now = act[:, 1 : 1 + piece].reshape(F_DEV, channels)
    keep_prev = (mine[:, :piece] == mine[:, 1 : 1 + piece])[:, :, None]
    keep_next = (mine[:, 2:] == mine[:, 1 : 1 + piece])[:, :, None]
    prev = jnp.where(keep_prev, act[:, :piece], jnp.zeros((), BF)).reshape(F_DEV, channels)
    nxt = jnp.where(keep_next, act[:, 2:], jnp.zeros((), BF)).reshape(F_DEV, channels)

    out_width = up_weight.shape[2]
    early = jnp.transpose(rising[0], (2, 1, 0, 3, 4))
    late = jnp.transpose(rising[1], (2, 0, 1, 3, 4))
    early = early.reshape(8, channels, out_width)
    late = late.reshape(8, channels, out_width)
    upsampled = upsample(now, prev, nxt, early, late)
    return upsampled.reshape(1, 1, groups, -1, out_width)


def upsample_kernel(now, prev, nxt, early, late, out, total):
    f32 = jnp.float32
    for r in range(8):
        if r < 4:
            value = jnp.dot(now[...], early[r + 4], preferred_element_type=f32)
            value += jnp.dot(prev[...], late[r + 4], preferred_element_type=f32)
        else:
            value = jnp.dot(now[...], late[r - 4], preferred_element_type=f32)
            value += jnp.dot(nxt[...], early[r - 4], preferred_element_type=f32)
        total[:, r, :] = value
    out[...] = total[...].astype(out.dtype)


def upsample(now, prev, nxt, early, late):
    frames, channels = now.shape
    width = early.shape[2]
    rows = 64
    tile = pl.BlockSpec((rows, channels), lambda i: (i, 0))
    whole = pl.BlockSpec((8, channels, width), lambda i: (0, 0, 0))
    return pl.pallas_call(
        upsample_kernel,
        grid=(frames // rows,),
        out_shape=jax.ShapeDtypeStruct((frames, 8, width), BF),
        in_specs=[tile, tile, tile, whole, whole],
        out_specs=pl.BlockSpec((rows, 8, width), lambda i: (i, 0, 0)),
        scratch_shapes=[pltpu.VMEM((rows, 8, width), jnp.float32)],
        name="upsample",
    )(now, prev, nxt, early, late)


def solution(mesh):
    placed = (
        P("utt", "tm"),
        P("utt", None),
        P("utt", None),
        P("utt", None),
        P("utt", "tm", None),
        P(),
        P(None, "tm"),
        P(None, "tm"),
        P(),
        P(),
        P(),
        P("tm", None, None),
    )
    return jax.shard_map(
        shards,
        mesh=mesh,
        in_specs=placed,
        out_specs=P("utt", "tm", None, None, None),
        check_vma=False,
    )
```

time: 335 us -> 148 us (0.44)
  waiting for transfers between devices: 117 us -> 0.01 us
  Pallas kernels: 0 us -> 99.1 us
  blocking collectives: 73.4 us -> 0 us
  other arithmetic: 84.5 us -> 13.5 us
  between operations: 13.5 us -> 0.32 us
  local copies, waits for them, and re-layouts: 23.8 us -> 13.6 us
    all_gather x3 -> x0, waiting for transfers between devices: 113 us -> none  [the longest x1 69.4 us: shards(): portion = lax.all_gather(up_weight, 'tm', axis=0, tiled=True)]
    pallas_call x0 -> x3, Pallas kernels: none -> 99.1 us  [the longest x2 92.1 us: gather_blocks(): pl.pallas_call(functools.partial(gather_kernel, count, share), out_shape=...]
    add x3, other arithmetic: 80 us -> 0.84 us  [the longest x1 0.68 us: shards(): mel_block = jnp.pad(mel_ph, ((0, 0), (0, WIDE - mel_width))) + told]
    all_gather x1 -> x0, blocking collectives: 48.4 us -> none  [shards(): outward = lax.all_gather(conv2_weight, 'tm', axis=1, tiled=True)]
    all_to_all x1 -> x0, blocking collectives: 25 us -> none  [shards(): lax.all_to_all(outgoing, 'utt', split_axis=0, concat_axis=0, tiled=True)]
    unnamed x20 -> x12, local copies, waits for them, and re-layouts: 14.8 us -> 1.64 us
    transpose x0 -> x3, local copies, waits for them, and re-layouts: none -> 5.93 us  [the longest x2 4.3 us: shards(): late = jnp.transpose(rising[1], (2, 0, 1, 3, 4))]
    gather x8 -> x0, local copies, waits for them, and re-layouts: 5.69 us -> none  [the longest x4 2.85 us: frame_layout(): jnp.take(offsets, owners) + exclusive - jnp.take(first_frame, owners)]
  transfers between devices with their start and end apart: 7 -> 3, of which waited for: 3 -> 0; matrix products, arithmetic and copies ran while one was open for 31% -> 15% of each run, Pallas kernels for 0% -> 44%
where the time goes in v1:
time: 148 us; the launch traced here: 147 us
  Pallas kernels  99.1 us (67%)
  local copies, waits for them, and re-layouts  13.6 us (9%)
  other arithmetic  13.5 us (9%)
  starting transfers between devices  11 us (7%)
  matrix products  9.53 us (6%)
    pallas_call x2, Pallas kernels, gather_blocks(): pl.pallas_call(functools.partial(gather_kernel, count, share), out_shape=...  92.1 us
    pallas_call x1, Pallas kernels, upsample(): pl.pallas_call(upsample_kernel, grid=(frames // rows,), out_shape=jax.Sha...  6.95 us
    dot_general x1, matrix products, shards(): conv_out = jnp.dot(filters, outward, preferred_element_type=jnp.float32)  5.6 us
    all_to_all x1, starting transfers between devices, shards(): lax.all_to_all(windows.reshape(groups, span, WIDE), 'utt', split_axis=0,...  4.92 us
    ppermute x1, starting transfers between devices, shards(): lax.ppermute(phone_ids[0, -4:], 'tm', [(i, i + 1) for i in range(ends)])  4.8 us
    transpose x2, local copies, waits for them, and re-layouts, shards(): late = jnp.transpose(rising[1], (2, 0, 1, 3, 4))  4.3 us
    dot_general x1, matrix products, shards(): jnp.dot(hit.astype(BF), portion, preferred_element_type=jnp.float32)  3.07 us
  transfers between devices with their start and end apart: 3, of which 0 were waited for; matrix products, arithmetic and copies ran while one was open for 15% of the time, Pallas kernels for 44%

profile of v1, /device:TPU:1, one launch (start us, length us, event | category | flops | bytes accessed | tf_op | source)
XLA Modules:
  0.0 147.0 jit_solution(11249639989867349130)
XLA Ops:
  0.0 0.8 slice_bitcast_fusion.3
  0.8 4.8 %collective-permute-start = (s32[4]{0:T(128)S(1)}, s32[4]{0:T(128)S(1)}, u32[]{:S(2)}, u32[]{:S(2)}) collective-permute-start(s32[4]{0:T(128)S(1)} %get-tuple-element.40), channel_id=1, source_target_pairs={{0,1},{1,2},{2,3},{3,4},{4,5},{5,6},{6,7},{7,8},{8,9},{9,10},{10,1... | collective-permute-start | bytes 56 | tf_op jit(solution)/shard_map/ppermute | solution.py:224
  5.6 1.3 collective-permute-start.1
  6.9 0.7 copy.50
  7.7 0.1 reduce-window.18
  7.8 0.1 reduce.2
  7.9 0.1 convert_reduce_fusion
  8.2 0.7 compare_select_fusion.1
  8.8 0.7 fusion.40
  9.5 1.0 reduce-window.11
  10.6 0.9 reshape.179
  11.6 0.9 copy.61
  12.4 0.6 fusion.24.refs_0_
  13.1 0.6 slice_select_fusion.17.refs_2_
  13.7 0.7 reshape.180
  14.4 0.6 fusion.38.refs_1_
  15.1 0.1 slice_reduce_fusion
  15.2 0.8 fusion.44
  16.1 0.8 select_reduce_fusion.2
  16.8 0.8 gather_fusion.1
  17.6 0.8 gather_fusion
  18.4 0.2 select_reduce_fusion.1
  18.6 0.3 select_reduce_fusion
  18.9 0.1 copy.48
  19.1 0.6 broadcast.155
  19.7 1.4 reduce.8
  21.2 0.1 fusion.43
  21.5 0.8 select_reduce_fusion.3
  22.3 0.1 add.106
  22.4 65.2 %gather1.1 = (bf16[2,8,8,8,3456]{4,3,2,1,0:T(8,128)(2,1)}, bf16[2,8,8,8,384]{4,3,2,1,0:T(8,128)(2,1)}, bf16[2,8,8,8,8,256]{5,4,3,2,1,0:T(8,128)(2,1)}) custom-call(bf16[8,3456]{1,0:T(8,128)(2,1)} %fusion.24.refs_0_, bf16[8,384]{1,0:T(8,128)(2,1)} %fusion.38.refs_1_, bf16[8,8,256]{2,1,0:T(8,128)(2,1)} %slice_select_fusion.17.refs_2_), custom_call_target="tpu_custom_call" | custom-call | tf_op jit(solution)/shard_map/gather1/pallas_call | solution.py:143
  87.7 0.7 pad_add_fusion
  88.4 0.2 convolution_convert_fusion
  88.6 0.1 fusion.32
  88.7 0.1 fusion.31
  88.8 0.1 fusion.30
  88.9 0.1 fusion.29
  89.0 0.1 fusion.28
  89.1 0.1 fusion.27
  89.2 0.1 fusion.26
  89.3 0.1 fusion.25
  89.4 5.6 %fusion.45 = (f32[64]{0:T(128)S(1)}, f32[64,384]{1,0:T(8,128)S(1)}) fusion(bf16[1024,384]{1,0:T(8,128)(2,1)} %bitcast.73, bf16[64,3456]{1,0:T(8,128)(2,1)S(1)} %fusion.25, bf16[1024,3456]{1,0:T(8,128)(2,1)} %bitcast.67, bf16[72,384]{1,0:T(8,128)(2,1)S(1)} %convolution_convert_fusion), kind=kOutput, calls=%fused_computation.129 | convolution fusion | flops 503521216 | bytes 8454400 | tf_op jit(solution)/shard_map/dot_general | solution.py:241
  95.0 0.2 multiply_reduce_fusion
  95.2 0.2 convolution_convert_fusion.1
  95.4 0.7 select_add_fusion.refs_0_
  96.1 26.9 %gather2.1 = bf16[1,8,8,64,128]{4,3,2,1,0:T(8,128)(2,1)} custom-call(bf16[64,128]{1,0:T(8,128)(2,1)} %select_add_fusion.refs_0_), custom_call_target="tpu_custom_call" | custom-call | tf_op jit(solution)/shard_map/gather2/pallas_call | solution.py:143
  123.0 3.1 %fusion.9 = bf16[320,128]{1,0:T(8,128)(2,1)} fusion(bf16[4096,128]{1,0:T(8,128)(2,1)} %bitcast.68, s32[4096]{0:T(1024)S(1)} %lt.41, s32[4096]{0:T(1024)S(1)} %ge.27, s32[320]{0:T(512)S(1)} %add.106), kind=kOutput, calls=%fused_computation.15 | convolution fusion | flops 339517440 | bytes 1164544 | tf_op jit(solution)/shard_map/dot_general | solution.py:272
  126.1 4.9 %all-to-all-start = ((bf16[8,40,128]{2,1,0:T(8,128)(2,1)}), bf16[8,40,128]{2,1,0:T(8,128)(2,1)S(1)}, u32[]{:S(2)}, u32[]{:S(2)}) async-start(bf16[8,40,128]{2,1,0:T(8,128)(2,1)} %bitcast.22), calls=%async_computation | async-start | bytes 163840 | tf_op jit(solution)/shard_map/all_to_all | solution.py:273
  131.0 2.7 %slice_bitcast_fusion = (bf16[8,8,8,8,256]{4,3,0,2,1:T(8,128)(2,1)S(1)}, bf16[8,8,8,8,256]{4,3,0,1,2:T(8,128)(2,1)S(1)}) fusion(bf16[2,8,8,8,8,256]{5,4,3,2,1,0:T(8,128)(2,1)} %get-tuple-element.11), kind=kLoop, calls=%fused_computation.9 | loop fusion | bytes 8388608 | tf_op jit(solution)/shard_map/transpose | solution.py:297
  133.7 1.6 %copy.55 = bf16[8,8,8,8,256]{4,3,2,1,0:T(8,128)(2,1)} copy(bf16[8,8,8,8,256]{4,3,0,1,2:T(8,128)(2,1)S(1)} %get-tuple-element.17) | data formatting | bytes 4194304 | tf_op jit(solution)/shard_map/transpose | solution.py:296
  135.4 1.6 %copy.56 = bf16[8,8,8,8,256]{4,3,2,1,0:T(8,128)(2,1)} copy(bf16[8,8,8,8,256]{4,3,0,2,1:T(8,128)(2,1)S(1)} %get-tuple-element.16) | data formatting | bytes 4194304 | tf_op jit(solution)/shard_map/transpose | solution.py:297
  137.0 0.1 slice.231
  137.1 0.1 copy.57
  137.4 0.1 fusion.22
  137.6 0.1 fusion.21
  137.7 0.1 fusion.20
  137.8 0.1 fusion.19
  138.0 0.1 fusion.18
  138.1 0.1 fusion.17
  138.2 0.1 fusion.16
  138.4 0.1 reshape.185
  138.5 0.5 fusion.14
  139.0 0.1 reshape.187
  139.1 1.0 slice_select_fusion
  140.1 6.9 %upsample.1 = bf16[256,8,256]{2,1,0:T(8,128)(2,1)} custom-call(bf16[256,512]{1,0:T(8,128)(2,1)} %bitcast.71, bf16[256,512]{1,0:T(8,128)(2,1)} %bitcast.70, bf16[256,512]{1,0:T(8,128)(2,1)} %bitcast.69, bf16[8,512,256]{2,1,0:T(8,128)(2,1)} %bitcast.65, bf16[8,512,256]{2,1,0:T(8,128)(2,1)} %bitcast.66), custom_call_target="tpu_custom_call" | custom-call | tf_op jit(solution)/shard_map/upsample/pallas_call | solution.py:323
  (39 shorter events, 1.2 us)
Async XLA Ops:
  0.0 88.4 %copy-start = (bf16[256,384]{1,0:T(8,128)(2,1)S(1)}, bf16[256,384]{1,0:T(8,128)(2,1)}, u32[]{:S(2)}) copy-start(bf16[256,384]{1,0:T(8,128)(2,1)} %param.19) | copy-start | bytes 589828
  0.8 86.8 %collective-permute-start = (s32[4]{0:T(128)S(1)}, s32[4]{0:T(128)S(1)}, u32[]{:S(2)}, u32[]{:S(2)}) collective-permute-start(s32[4]{0:T(128)S(1)} %get-tuple-element.40), channel_id=1, source_target_pairs={{0,1},{1,2},{2,3},{3,4},{4,5},{5,6},{6,7},{7,8},{8,9},{9,10},{10,1... | collective-permute-start | bytes 56 | tf_op jit(solution)/shard_map/ppermute | solution.py:224
  5.6 82.0 %collective-permute-start.1 = (s32[4]{0:T(128)S(1)}, s32[4]{0:T(128)S(1)}, u32[]{:S(2)}, u32[]{:S(2)}) collective-permute-start(s32[4]{0:T(128)S(1)} %get-tuple-element.41), channel_id=1, source_target_pairs={{1,0},{2,1},{3,2},{4,3},{5,4},{6,5},{7,6},{8,7},{9,8},{10,9},{11,1... | collective-permute-start | bytes 56 | tf_op jit(solution)/shard_map/ppermute | solution.py:223
  89.3 5.8 %copy-start.2 = (bf16[384,80]{0,1:T(8,128)(2,1)S(1)}, bf16[384,80]{0,1:T(8,128)(2,1)}, u32[]{:S(2)}) copy-start(bf16[384,80]{0,1:T(8,128)(2,1)} %param.23) | copy-start | bytes 184324
  89.4 5.8 %copy-start.3 = (f32[384]{0:T(512)S(1)}, f32[384]{0:T(512)}, u32[]{:S(2)}) copy-start(f32[384]{0:T(512)} %param.22) | copy-start | bytes 4612
  126.1 11.0 %all-to-all-start = ((bf16[8,40,128]{2,1,0:T(8,128)(2,1)}), bf16[8,40,128]{2,1,0:T(8,128)(2,1)S(1)}, u32[]{:S(2)}, u32[]{:S(2)}) async-start(bf16[8,40,128]{2,1,0:T(8,128)(2,1)} %bitcast.22), calls=%async_computation | async-start | bytes 163840 | tf_op jit(solution)/shard_map/all_to_all | solution.py:273
  133.7 3.2 %copy-start.1 = (bf16[7,80,512]{2,1,0:T(8,128)(2,1)S(1)}, bf16[7,80,512]{2,1,0:T(8,128)(2,1)}, u32[]{:S(2)}) copy-start(bf16[7,80,512]{2,1,0:T(8,128)(2,1)} %param.24) | copy-start | bytes 1720324

commit v2 on v1

--- a/solution.py
+++ b/solution.py
@@ -16,10 +16,11 @@
 BF = jnp.bfloat16
 
 
-def gather_kernel(count, share, *refs):
+def gather_kernel(count, share, swap, *refs):
     blocks = refs[:count]
-    outs = refs[count : 2 * count]
-    local_sem, first_send, first_recv, ring_send, ring_recv, pair_send, pair_recv = refs[2 * count :]
+    outs = refs[count + swap : 2 * count + swap]
+    scratch = refs[2 * (count + swap) :]
+    local_sem, first_send, first_recv, ring_send, ring_recv, pair_send, pair_recv = scratch[:7]
     utt = lax.axis_index("utt")
     tm = lax.axis_index("tm")
     core = lax.rem(utt, 2)
@@ -47,9 +48,9 @@
     down = lax.rem(second + SIDE - 1, SIDE)
     for side in (up, down):
         pl.semaphore_signal(barrier, inc=1, device_id=(utt, place(first, side)), device_id_type=MESH)
-    if share:
+    if share or swap:
         pl.semaphore_signal(barrier, inc=1, device_id=(pair, tm), device_id_type=MESH)
-    pl.semaphore_wait(barrier, SIDE + 1 + (1 if share else 0))
+    pl.semaphore_wait(barrier, SIDE + 1 + (1 if share or swap else 0))
 
     own = [
         pltpu.make_async_copy(blocks[i], outs[i].at[half, second, first], local_sem.at[i])
@@ -71,6 +72,23 @@
     for i in range(count):
         for step in range(1, SIDE):
             first_copy(i, step).start()
+    swaps = []
+    if swap:
+        given, taken = refs[count], refs[2 * count + 1]
+        pieces = scratch[7].shape[0]
+        length = given.shape[0] // pieces
+        for number in range(pieces):
+            rows = pl.ds(number * length, length)
+            copy = pltpu.make_async_remote_copy(
+                src_ref=given.at[rows],
+                dst_ref=taken.at[rows],
+                send_sem=scratch[7].at[number],
+                recv_sem=scratch[8].at[number],
+                device_id=(pair, tm),
+                device_id_type=MESH,
+            )
+            copy.start()
+            swaps.append(copy)
     for copy in own:
         copy.wait()
     for i in range(count):
@@ -135,30 +153,43 @@
                 ring_copy(i, way, step).wait_send()
     for copy in pairs:
         copy.wait_send()
-
-
-def gather_blocks(blocks, share, number):
+    for copy in swaps:
+        copy.wait()
+
+
+def gather_blocks(blocks, share, number, space, swapped=None):
     count = len(blocks)
     halves = 2 if share else 1
+    swap = 0 if swapped is None else 1
+    scratch = [
+        pltpu.SemaphoreType.DMA((count,)),
+        pltpu.SemaphoreType.DMA((count, SIDE)),
+        pltpu.SemaphoreType.DMA((count, SIDE)),
+        pltpu.SemaphoreType.DMA((count, 2, SIDE // 2)),
+        pltpu.SemaphoreType.DMA((count, 2, SIDE // 2)),
+        pltpu.SemaphoreType.DMA((count, SIDE)),
+        pltpu.SemaphoreType.DMA((count, SIDE)),
+    ]
+    shapes = [
+        jax.ShapeDtypeStruct((halves, SIDE, SIDE) + block.shape, block.dtype) for block in blocks
+    ]
+    operands = list(blocks)
+    if swap:
+        scratch += [pltpu.SemaphoreType.DMA((4,)), pltpu.SemaphoreType.DMA((4,))]
+        shapes.append(jax.ShapeDtypeStruct(swapped.shape, swapped.dtype))
+        operands.append(swapped)
+    specs = [pl.BlockSpec(memory_space=space)] * count
+    specs += [pl.BlockSpec(memory_space=pl.ANY)] * swap
     return pl.pallas_call(
-        functools.partial(gather_kernel, count, share),
-        out_shape=[
-            jax.ShapeDtypeStruct((halves, SIDE, SIDE) + block.shape, block.dtype) for block in blocks
-        ],
-        in_specs=[pl.BlockSpec(memory_space=pl.ANY)] * count,
-        out_specs=[pl.BlockSpec(memory_space=pl.ANY)] * count,
-        scratch_shapes=[
-            pltpu.SemaphoreType.DMA((count,)),
-            pltpu.SemaphoreType.DMA((count, SIDE)),
-            pltpu.SemaphoreType.DMA((count, SIDE)),
-            pltpu.SemaphoreType.DMA((count, 2, SIDE // 2)),
-            pltpu.SemaphoreType.DMA((count, 2, SIDE // 2)),
-            pltpu.SemaphoreType.DMA((count, SIDE)),
-            pltpu.SemaphoreType.DMA((count, SIDE)),
-        ],
+        functools.partial(gather_kernel, count, share, swap),
+        out_shape=shapes,
+        in_specs=specs,
+        out_specs=specs,
+        scratch_shapes=scratch,
         compiler_params=pltpu.CompilerParams(collective_id=number, has_side_effects=True),
+        cost_estimate=pl.CostEstimate(flops=0, bytes_accessed=100_000_000, transcendentals=0),
         name=f"gather{number}",
-    )(*blocks)
+    )(*operands)
 
 
 def utterance_of(indices, bounds):
@@ -204,14 +235,19 @@
     core = lax.rem(lax.axis_index("utt"), 2)
     ends = lax.axis_size("tm") - 1
 
+    symbols = embed_table.shape[0]
     filters_here = conv1_weight.shape[1]
     part = filters_here // 2
-    pad = ((0, 0), (0, 8 - part), (0, 0))
-    inward = jnp.pad(conv1_weight.T.reshape(2, part, -1), pad)
-    outward = jnp.pad(conv2_weight.T.reshape(2, part, -1), pad)
-    rising = jnp.transpose(up_weight, (1, 0, 2)).reshape(2, 8, up_weight.shape[0], -1)
     pick = lambda both: jnp.where(core == 0, both[0], both[1])
-    inward, outward, rising = gather_blocks([pick(inward), pick(outward), pick(rising)], True, 1)
+    rising = pick(jnp.transpose(up_weight, (1, 0, 2)).reshape(2, 8, up_weight.shape[0], -1))
+    own_taps = lax.all_gather(rising, "tm", axis=1, tiled=True)
+    inward = pick(conv1_weight.T.reshape(2, part, -1)).reshape(part * 9, width)
+    inward = lax.dot_general(
+        inward, embed_table, (((1,), (1,)), ((), ())), preferred_element_type=jnp.float32
+    ).astype(BF)
+    inward = jnp.pad(inward.reshape(part, 9 * symbols), ((0, 8 - part), (0, 0)))
+    outward = jnp.pad(pick(conv2_weight.T.reshape(2, part, -1)), ((0, 8 - part), (0, 0)))
+    inward, outward = gather_blocks([inward, outward], True, 1, pl.ANY)
     rows = 2 * SIDE * SIDE * 8
     inward = inward.reshape(rows, -1)
     outward = outward.reshape(rows, -1)
@@ -223,14 +259,14 @@
     head = lax.ppermute(phone_ids[0, :4], "tm", [(i + 1, i) for i in range(ends)])
     tail = lax.ppermute(phone_ids[0, -4:], "tm", [(i, i + 1) for i in range(ends)])
     ids = jnp.concatenate([tail, phone_ids[0], head])
-    symbols = embed_table.shape[0]
-    choose = (ids[:, None] == jnp.arange(symbols, dtype=jnp.int32)[None, :]).astype(BF)
-    widened = jnp.dot(choose, embed_table, preferred_element_type=jnp.float32).astype(BF)
+    table = jnp.arange(symbols, dtype=jnp.int32)[None, :]
+    chosen = (phone_ids[0][:, None] == table).astype(BF)
+    embedded = jnp.dot(chosen, embed_table, preferred_element_type=jnp.float32)
     center = phone_labels[4 : 4 + phone_count]
     columns = []
     for tap in range(9):
-        keep = (phone_labels[tap : tap + phone_count] == center)[:, None]
-        columns.append(jnp.where(keep, widened[tap : tap + phone_count], jnp.zeros((), BF)))
+        keep = phone_labels[tap : tap + phone_count] == center
+        columns.append((jnp.where(keep, ids[tap : tap + phone_count], -1)[:, None] == table).astype(BF))
     unfolded = jnp.concatenate(columns, axis=1)
     filters = jnp.maximum(
         lax.dot_general(
@@ -239,7 +275,7 @@
         0.0,
     ).astype(BF)
     conv_out = jnp.dot(filters, outward, preferred_element_type=jnp.float32)
-    resid = widened[4 : 4 + phone_count].astype(jnp.float32) + conv_out
+    resid = embedded + conv_out
     middle = jnp.mean(resid, axis=1, keepdims=True)
     spread = jnp.mean((resid - middle) ** 2, axis=1, keepdims=True)
     decoded = ((resid - middle) * lax.rsqrt(spread + EPS) * norm_gain[None, :]).astype(BF)
@@ -248,7 +284,7 @@
     lane = lax.broadcasted_iota(jnp.int32, (phone_count, WIDE), 1)
     told = jnp.where(lane == mel_width, (center + 1).astype(BF)[:, None], jnp.zeros((), BF))
     mel_block = jnp.pad(mel_ph, ((0, 0), (0, WIDE - mel_width))) + told
-    (portion,) = gather_blocks([mel_block], False, 2)
+    portion, other_taps = gather_blocks([mel_block], False, 2, pltpu.VMEM, own_taps)
     portion = portion.reshape(-1, WIDE)
 
     def arranged(values):
@@ -293,24 +329,32 @@
     nxt = jnp.where(keep_next, act[:, 2:], jnp.zeros((), BF)).reshape(F_DEV, channels)
 
     out_width = up_weight.shape[2]
-    early = jnp.transpose(rising[0], (2, 1, 0, 3, 4))
-    late = jnp.transpose(rising[1], (2, 0, 1, 3, 4))
-    early = early.reshape(8, channels, out_width)
-    late = late.reshape(8, channels, out_width)
-    upsampled = upsample(now, prev, nxt, early, late)
+    upsampled = upsample(now, prev, nxt, own_taps, other_taps)
     return upsampled.reshape(1, 1, groups, -1, out_width)
 
 
-def upsample_kernel(now, prev, nxt, early, late, out, total):
+def upsample_kernel(now, prev, nxt, own, other, out, total):
     f32 = jnp.float32
-    for r in range(8):
-        if r < 4:
-            value = jnp.dot(now[...], early[r + 4], preferred_element_type=f32)
-            value += jnp.dot(prev[...], late[r + 4], preferred_element_type=f32)
-        else:
-            value = jnp.dot(now[...], late[r - 4], preferred_element_type=f32)
-            value += jnp.dot(nxt[...], early[r - 4], preferred_element_type=f32)
-        total[:, r, :] = value
+    core = lax.rem(lax.axis_index("utt"), 2)
+
+    def run(early, late):
+        for r in range(8):
+            if r < 4:
+                value = jnp.dot(now[...], early[r + 4], preferred_element_type=f32)
+                value += jnp.dot(prev[...], late[r + 4], preferred_element_type=f32)
+            else:
+                value = jnp.dot(now[...], late[r - 4], preferred_element_type=f32)
+                value += jnp.dot(nxt[...], early[r - 4], preferred_element_type=f32)
+            total[:, r, :] = value
+
+    @pl.when(core == 0)
+    def _():
+        run(own, other)
+
+    @pl.when(core == 1)
+    def _():
+        run(other, own)
+
     out[...] = total[...].astype(out.dtype)
 
 

time: 148 us -> 164 us (1.11)
  waiting for transfers between devices: 0.01 us -> 18.3 us
  Pallas kernels: 99.1 us -> 83.5 us
  between operations: 0.32 us -> 13.7 us
  local copies, waits for them, and re-layouts: 13.6 us -> 7.22 us
  starting transfers between devices: 11 us -> 15.9 us
    pallas_call x2, Pallas kernels: 92.1 us -> 76.5 us  [gather_blocks(): pl.pallas_call(functools.partial(gather_kernel, count, share, swap), out_...]
    all_gather x0 -> x1, waiting for transfers between devices: none -> 13.5 us  [shards(): own_taps = lax.all_gather(rising, 'tm', axis=1, tiled=True)]
    transpose x3 -> x0, local copies, waits for them, and re-layouts: 5.93 us -> none  [the longest x2 4.3 us: shards(): late = jnp.transpose(rising[1], (2, 0, 1, 3, 4))]
    all_to_all x1, starting transfers between devices: 4.92 us -> 9.76 us  [shards(): lax.all_to_all(windows.reshape(groups, span, WIDE), 'utt', split_axis=0,...]
    all_to_all x1, waiting for transfers between devices: 0.01 us -> 4.84 us  [shards(): lax.all_to_all(windows.reshape(groups, span, WIDE), 'utt', split_axis=0,...]
    unnamed x14 -> x15, other arithmetic: 2.83 us -> 3.51 us
  transfers between devices with their start and end apart: 3 -> 4, of which waited for: 0 -> 2; matrix products, arithmetic and copies ran while one was open for 15% -> 15% of each run, Pallas kernels for 44% -> 30%
where the time goes in v2:
time: 164 us; the launch traced here: 163 us
  Pallas kernels  83.5 us (51%)
  waiting for transfers between devices  18.3 us (11%)
  starting transfers between devices  15.9 us (10%)
  other arithmetic  14.9 us (9%)
  between operations  13.7 us (8%)
  matrix products  9.25 us (6%)
  local copies, waits for them, and re-layouts  7.22 us (4%)
    pallas_call x2, Pallas kernels, gather_blocks(): pl.pallas_call(functools.partial(gather_kernel, count, share, swap), out_...  76.5 us
    all_gather x1, waiting for transfers between devices, shards(): own_taps = lax.all_gather(rising, 'tm', axis=1, tiled=True)  13.5 us
    all_to_all x1, starting transfers between devices, shards(): lax.all_to_all(windows.reshape(groups, span, WIDE), 'utt', split_axis=0,...  9.76 us
    pallas_call x1, Pallas kernels, upsample(): pl.pallas_call(upsample_kernel, grid=(frames // rows,), out_shape=jax.Sha...  6.97 us
    all_to_all x1, waiting for transfers between devices, shards(): lax.all_to_all(windows.reshape(groups, span, WIDE), 'utt', split_axis=0,...  4.84 us
    ppermute x1, starting transfers between devices, shards(): lax.ppermute(phone_ids[0, -4:], 'tm', [(i, i + 1) for i in range(ends)])  4.8 us
    dot_general x1, matrix products, shards(): conv_out = jnp.dot(filters, outward, preferred_element_type=jnp.float32)  4.4 us
    unnamed x15, other arithmetic  3.51 us
  transfers between devices with their start and end apart: 4, of which 2 were waited for; matrix products, arithmetic and copies ran while one was open for 15% of the time, Pallas kernels for 30%

profile of v2, /device:TPU:1, one launch (start us, length us, event | category | flops | bytes accessed | tf_op | source)
XLA Modules:
  0.0 162.7 jit_solution(9285670554019686321)
XLA Ops:
  6.5 0.8 slice_bitcast_fusion
  7.3 4.8 %collective-permute-start = (s32[4]{0:T(128)S(1)}, s32[4]{0:T(128)S(1)}, u32[]{:S(2)}, u32[]{:S(2)}) collective-permute-start(s32[4]{0:T(128)S(1)} %get-tuple-element.44), channel_id=1, source_target_pairs={{0,1},{1,2},{2,3},{3,4},{4,5},{5,6},{6,7},{7,8},{8,9},{9,10},{10,1... | collective-permute-start | bytes 56 | tf_op jit(solution)/shard_map/ppermute | solution.py:260
  12.2 1.3 collective-permute-start.1
  13.5 0.9 copy.53
  14.4 0.6 slice_select_fusion.10
  15.0 0.7 copy.44
  15.7 0.1 reduce-window.18
  15.8 0.1 reduce.2
  15.9 0.7 compare_select_fusion.1
  16.6 0.7 fusion.38
  17.3 1.0 reduce-window.11
  18.4 0.1 convert_reduce_fusion
  18.5 1.0 slice_select_fusion.9
  19.6 0.8 slice_select_fusion.11
  20.4 0.2 convolution_convert_fusion
  20.6 0.9 fusion.24
  21.5 0.1 slice_reduce_fusion
  21.6 0.1 reshape.178
  21.7 0.8 fusion.42
  22.5 0.8 select_reduce_fusion.2
  23.3 0.8 gather_fusion.1
  24.1 0.8 gather_fusion
  24.9 0.2 select_reduce_fusion.1
  25.1 0.3 select_reduce_fusion
  25.4 0.1 copy.42
  25.6 0.5 broadcast.157
  26.1 1.4 reduce.8
  27.6 0.8 select_reduce_fusion.3
  28.6 0.6 pad.16.refs_0_
  29.2 0.6 pad.17.refs_1_
  30.0 49.2 %gather1.1 = (bf16[2,8,8,8,2304]{4,3,2,1,0:T(8,128)(2,1)}, bf16[2,8,8,8,384]{4,3,2,1,0:T(8,128)(2,1)}) custom-call(bf16[8,2304]{1,0:T(8,128)(2,1)} %pad.16.refs_0_, bf16[8,384]{1,0:T(8,128)(2,1)} %pad.17.refs_1_), custom_call_target="tpu_custom_call" | custom-call | bytes 100000000 | tf_op jit(solution)/shard_map/gather1/pallas_call | solution.py:183
  79.2 0.8 pad_add_fusion.1
  80.2 0.1 fusion.25
  80.3 0.1 fusion.26
  80.4 0.1 fusion.27
  80.5 0.1 fusion.28
  80.6 0.7 fusion.23
  81.3 0.1 fusion.29
  81.4 0.1 fusion.30
  81.5 0.1 fusion.31
  81.6 0.1 fusion.32
  81.7 4.4 %fusion.43 = (f32[64]{0:T(128)S(1)}, f32[64,384]{1,0:T(8,128)S(1)}) fusion(f32[64,384]{1,0:T(8,128)S(1)} %fusion.24, bf16[1024,384]{1,0:T(8,128)(2,1)} %bitcast.58, pred[64,2304]{1,0:T(8,128)(4,1)S(1)} %fusion.32, bf16[1024,2304]{1,0:T(8,128)(2,1)} %bitcast.53), kind=kOutput, calls=%fused_computation.123 | convolution fusion | flops 352501696 | bytes 5849344 | tf_op jit(solution)/shard_map/dot_general | solution.py:277
  86.1 0.2 multiply_reduce_fusion
  86.3 0.2 convolution_convert_fusion.1
  86.5 0.7 select_add_fusion.refs_0_
  87.2 13.5 %all-gather.2.cloned.1.call-done.refs_1_.own = bf16[8,512,256]{2,1,0:T(8,128)(2,1)} async-done(((bf16[8,8,256]{2,1,0:T(8,128)(2,1)}), bf16[8,512,256]{2,1,0:T(8,128)(2,1)}) %all-gather.2.cloned.1.call-update) | async-done | bytes 2097168 | tf_op jit(solution)/shard_map/all_gather | solution.py:243
  100.6 27.4 %gather2.1 = (bf16[1,8,8,64,128]{4,3,2,1,0:T(8,128)(2,1)}, bf16[8,512,256]{2,1,0:T(8,128)(2,1)}) custom-call(bf16[64,128]{1,0:T(8,128)(2,1)} %select_add_fusion.refs_0_, bf16[8,512,256]{2,1,0:T(8,128)(2,1)} %all-gather.2.cloned.1.call-done.refs_1_.own), custom_call_target="tpu_custom_call" | custom-call | bytes 100000000 | tf_op jit(solution)/shard_map/gather2/pallas_call | solution.py:183
  128.0 3.1 %fusion.9 = bf16[320,128]{1,0:T(8,128)(2,1)} fusion(bf16[4096,128]{1,0:T(8,128)(2,1)} %bitcast.71, s32[4096]{0:T(1024)S(1)} %lt.41, s32[4096]{0:T(1024)S(1)} %ge.27, s32[320]{0:T(512)S(1)} %add.106), kind=kOutput, calls=%fused_computation.13 | convolution fusion | flops 339517440 | bytes 1164544 | tf_op jit(solution)/shard_map/dot_general | solution.py:308
  131.1 9.8 %all-to-all-start = ((bf16[8,40,128]{2,1,0:T(8,128)(2,1)}), bf16[8,40,128]{2,1,0:T(8,128)(2,1)S(1)}, u32[]{:S(2)}, u32[]{:S(2)}) async-start(bf16[8,40,128]{2,1,0:T(8,128)(2,1)} %bitcast.20), calls=%async_computation | async-start | bytes 163840 | tf_op jit(solution)/shard_map/all_to_all | solution.py:309
  141.0 4.8 %all-to-all-done = bf16[8,40,128]{2,1,0:T(8,128)(2,1)S(1)} async-done(((bf16[8,40,128]{2,1,0:T(8,128)(2,1)}), bf16[8,40,128]{2,1,0:T(8,128)(2,1)S(1)}, u32[]{:S(2)}, u32[]{:S(2)}) %all-to-all-start) | async-done | bytes 81952 | tf_op jit(solution)/shard_map/all_to_all | solution.py:309
  145.8 0.1 slice.225
  145.9 0.1 copy.49
  146.2 0.1 fusion.22
  146.3 0.1 fusion.21
  146.5 0.1 fusion.20
  146.6 0.1 fusion.19
  146.7 0.1 fusion.18
  146.9 0.1 fusion.17
  147.0 0.1 fusion.16
  147.1 0.1 reshape.188
  147.3 0.5 fusion.14
  147.8 0.1 reshape.190
  147.8 1.1 slice_select_fusion
  148.9 7.0 %upsample.1 = bf16[256,8,256]{2,1,0:T(8,128)(2,1)} custom-call(bf16[256,512]{1,0:T(8,128)(2,1)} %bitcast.56, bf16[256,512]{1,0:T(8,128)(2,1)} %bitcast.55, bf16[256,512]{1,0:T(8,128)(2,1)} %bitcast.54, bf16[8,512,256]{2,1,0:T(8,128)(2,1)} %all-gather.2.cloned.1.call-done.refs_1_.own, bf16[8,512,256]{2,1,0:T(8,128)(2,1)} %get-tuple-element.13.other), custom_call_target="tpu_custom_call" | custom-call | tf_op jit(solution)/shard_map/upsample/pallas_call | solution.py:367
  (42 shorter events, 1.4 us)
Async XLA Ops:
  6.5 13.9 %copy-start = (bf16[256,384]{1,0:T(8,128)(2,1)S(1)}, bf16[256,384]{1,0:T(8,128)(2,1)}, u32[]{:S(2)}) copy-start(bf16[256,384]{1,0:T(8,128)(2,1)} %param.19) | copy-start | bytes 589828
  6.5 94.1 %all-gather.2.cloned.1.call-start = ((), (), s32[]{:S(2)}) async-start(), calls=%async_computation.1 | async-start | bytes 2129920 | tf_op jit(solution)/shard_map/all_gather | solution.py:243
  7.3 71.9 %collective-permute-start = (s32[4]{0:T(128)S(1)}, s32[4]{0:T(128)S(1)}, u32[]{:S(2)}, u32[]{:S(2)}) collective-permute-start(s32[4]{0:T(128)S(1)} %get-tuple-element.44), channel_id=1, source_target_pairs={{0,1},{1,2},{2,3},{3,4},{4,5},{5,6},{6,7},{7,8},{8,9},{9,10},{10,1... | collective-permute-start | bytes 56 | tf_op jit(solution)/shard_map/ppermute | solution.py:260
  12.2 67.1 %collective-permute-start.1 = (s32[4]{0:T(128)S(1)}, s32[4]{0:T(128)S(1)}, u32[]{:S(2)}, u32[]{:S(2)}) collective-permute-start(s32[4]{0:T(128)S(1)} %get-tuple-element.43), channel_id=1, source_target_pairs={{1,0},{2,1},{3,2},{4,3},{5,4},{6,5},{7,6},{8,7},{9,8},{10,9},{11,1... | collective-permute-start | bytes 56 | tf_op jit(solution)/shard_map/ppermute | solution.py:259
  14.3 71.9 %copy-start.2 = (bf16[384,80]{0,1:T(8,128)(2,1)S(1)}, bf16[384,80]{0,1:T(8,128)(2,1)}, u32[]{:S(2)}) copy-start(bf16[384,80]{0,1:T(8,128)(2,1)} %param.23) | copy-start | bytes 184324
  14.3 71.9 %copy-start.3 = (f32[384]{0:T(512)S(1)}, f32[384]{0:T(512)}, u32[]{:S(2)}) copy-start(f32[384]{0:T(512)} %param.22) | copy-start | bytes 4612
  128.0 12.9 %copy-start.1 = (bf16[7,80,512]{2,1,0:T(8,128)(2,1)S(1)}, bf16[7,80,512]{2,1,0:T(8,128)(2,1)}, u32[]{:S(2)}) copy-start(bf16[7,80,512]{2,1,0:T(8,128)(2,1)} %param.24) | copy-start | bytes 1720324
  131.1 14.7 %all-to-all-start = ((bf16[8,40,128]{2,1,0:T(8,128)(2,1)}), bf16[8,40,128]{2,1,0:T(8,128)(2,1)S(1)}, u32[]{:S(2)}, u32[]{:S(2)}) async-start(bf16[8,40,128]{2,1,0:T(8,128)(2,1)} %bitcast.20), calls=%async_computation | async-start | bytes 163840 | tf_op jit(solution)/shard_map/all_to_all | solution.py:309
Sparse Core Ops, SparseCore 0:
  15.1 85.4 all-gather.1

commit v3 on v1

--- a/solution.py
+++ b/solution.py
@@ -14,6 +14,9 @@
 EPS = 1e-05
 MESH = pl.DeviceIdType.MESH
 BF = jnp.bfloat16
+
+
+ORDER = (0, 1, 7, 2, 6, 3, 5, 4)
 
 
 def gather_kernel(count, share, *refs):
@@ -33,6 +36,9 @@
     def place(a, b):
         return a * SIDE + b + core * ((b - a) * SIDE + (a - b))
 
+    def beside(step):
+        return lax.rem(second + step + SIDE, SIDE)
+
     barrier = pltpu.get_barrier_semaphore()
 
     def greet(step, carry):
@@ -43,10 +49,10 @@
         return carry
 
     lax.fori_loop(1, SIDE, greet, 0)
-    up = lax.rem(second + 1, SIDE)
-    down = lax.rem(second + SIDE - 1, SIDE)
-    for side in (up, down):
-        pl.semaphore_signal(barrier, inc=1, device_id=(utt, place(first, side)), device_id_type=MESH)
+    for side in (1, -1):
+        pl.semaphore_signal(
+            barrier, inc=1, device_id=(utt, place(first, beside(side))), device_id_type=MESH
+        )
     if share:
         pl.semaphore_signal(barrier, inc=1, device_id=(pair, tm), device_id_type=MESH)
     pl.semaphore_wait(barrier, SIDE + 1 + (1 if share else 0))
@@ -55,8 +61,6 @@
         pltpu.make_async_copy(blocks[i], outs[i].at[half, second, first], local_sem.at[i])
         for i in range(count)
     ]
-    for copy in own:
-        copy.start()
 
     def first_copy(i, step):
         return pltpu.make_async_remote_copy(
@@ -68,78 +72,79 @@
             device_id_type=MESH,
         )
 
-    for i in range(count):
-        for step in range(1, SIDE):
+    def ring_copy(i, way, step, order):
+        side = 1 - 2 * way
+        block = lax.rem(first - order + SIDE, SIDE)
+        spot = outs[i].at[half, beside(-side * step), block]
+        return pltpu.make_async_remote_copy(
+            src_ref=spot,
+            dst_ref=spot,
+            send_sem=ring_send.at[i, way, step, order],
+            recv_sem=ring_recv.at[i, way, step, order],
+            device_id=(utt, place(first, beside(side))),
+            device_id_type=MESH,
+        )
+
+    def pair_copy(i, step):
+        row = outs[i].at[half, beside(step)]
+        return pltpu.make_async_remote_copy(
+            src_ref=row,
+            dst_ref=row,
+            send_sem=pair_send.at[i, step + 3],
+            recv_sem=pair_recv.at[i, step + 3],
+            device_id=(pair, tm),
+            device_id_type=MESH,
+        )
+
+    def steps_of(way, order):
+        return SIDE // 2 - (order + way) % 2
+
+    for copy in own:
+        copy.start()
+    for step in ORDER[1:]:
+        for i in range(count):
             first_copy(i, step).start()
     for copy in own:
         copy.wait()
+    for order in ORDER:
+        for i in range(count):
+            if order > 0:
+                first_copy(i, order).wait_recv()
+            for way in range(2):
+                ring_copy(i, way, 0, order).start()
+    if share:
+        for i in range(count):
+            pair_copy(i, 0).start()
+    for step in range(SIDE // 2):
+        for order in ORDER:
+            for i in range(count):
+                for way in range(2):
+                    if step < steps_of(way, order):
+                        ring_copy(i, way, step, order).wait_recv()
+                        if step + 1 < steps_of(way, order):
+                            ring_copy(i, way, step + 1, order).start()
+        if share:
+            for i in range(count):
+                pair_copy(i, -step - 1 if step < 3 else 4).start()
+                if step < 3:
+                    pair_copy(i, step + 1).start()
     for i in range(count):
-        for step in range(1, SIDE):
-            first_copy(i, step).wait_recv()
-
-    def ring_copy(i, way, step):
-        slot = lax.rem(second - step + SIDE, SIDE) if way == 0 else lax.rem(second + step, SIDE)
-        row = outs[i].at[half, slot]
-        return pltpu.make_async_remote_copy(
-            src_ref=row,
-            dst_ref=row,
-            send_sem=ring_send.at[i, way, step],
-            recv_sem=ring_recv.at[i, way, step],
-            device_id=(utt, place(first, up if way == 0 else down)),
-            device_id_type=MESH,
-        )
-
-    def pair_copy(i, slot, number):
-        row = outs[i].at[half, slot]
-        return pltpu.make_async_remote_copy(
-            src_ref=row,
-            dst_ref=row,
-            send_sem=pair_send.at[i, number],
-            recv_sem=pair_recv.at[i, number],
-            device_id=(pair, tm),
-            device_id_type=MESH,
-        )
-
-    pairs = []
-
-    def hand_over(i, slot, number):
-        if share:
-            copy = pair_copy(i, slot, number)
-            copy.start()
-            pairs.append(copy)
-
-    ways = ((0, SIDE // 2), (1, SIDE // 2 - 1))
-    for i in range(count):
-        for way, _ in ways:
-            ring_copy(i, way, 0).start()
-        hand_over(i, second, 0)
-    for step in range(SIDE // 2):
+        for order in ORDER:
+            if order > 0:
+                first_copy(i, order).wait_send()
+            for way in range(2):
+                for step in range(steps_of(way, order)):
+                    ring_copy(i, way, step, order).wait_send()
+    if share:
         for i in range(count):
-            for way, steps in ways:
-                if step < steps:
-                    ring_copy(i, way, step).wait_recv()
-                    if step + 1 < steps:
-                        ring_copy(i, way, step + 1).start()
-                    if way == 0:
-                        slot = lax.rem(second - step - 1 + SIDE, SIDE)
-                    else:
-                        slot = lax.rem(second + step + 1, SIDE)
-                    hand_over(i, slot, 1 + 2 * step + way)
-    for copy in pairs:
-        copy.wait_recv()
-    for i in range(count):
-        for step in range(1, SIDE):
-            first_copy(i, step).wait_send()
-        for way, steps in ways:
-            for step in range(steps):
-                ring_copy(i, way, step).wait_send()
-    for copy in pairs:
-        copy.wait_send()
+            for step in range(-3, 5):
+                pair_copy(i, step).wait()
 
 
 def gather_blocks(blocks, share, number):
     count = len(blocks)
     halves = 2 if share else 1
+    ring = (count, 2, SIDE // 2, SIDE)
     return pl.pallas_call(
         functools.partial(gather_kernel, count, share),
         out_shape=[
@@ -151,8 +156,8 @@
             pltpu.SemaphoreType.DMA((count,)),
             pltpu.SemaphoreType.DMA((count, SIDE)),
             pltpu.SemaphoreType.DMA((count, SIDE)),
-            pltpu.SemaphoreType.DMA((count, 2, SIDE // 2)),
-            pltpu.SemaphoreType.DMA((count, 2, SIDE // 2)),
+            pltpu.SemaphoreType.DMA(ring),
+            pltpu.SemaphoreType.DMA(ring),
             pltpu.SemaphoreType.DMA((count, SIDE)),
             pltpu.SemaphoreType.DMA((count, SIDE)),
         ],
@@ -204,17 +209,22 @@
     core = lax.rem(lax.axis_index("utt"), 2)
     ends = lax.axis_size("tm") - 1
 
+    symbols = embed_table.shape[0]
     filters_here = conv1_weight.shape[1]
     part = filters_here // 2
-    pad = ((0, 0), (0, 8 - part), (0, 0))
-    inward = jnp.pad(conv1_weight.T.reshape(2, part, -1), pad)
-    outward = jnp.pad(conv2_weight.T.reshape(2, part, -1), pad)
-    rising = jnp.transpose(up_weight, (1, 0, 2)).reshape(2, 8, up_weight.shape[0], -1)
     pick = lambda both: jnp.where(core == 0, both[0], both[1])
-    inward, outward, rising = gather_blocks([pick(inward), pick(outward), pick(rising)], True, 1)
-    rows = 2 * SIDE * SIDE * 8
-    inward = inward.reshape(rows, -1)
-    outward = outward.reshape(rows, -1)
+    rising = pick(jnp.transpose(up_weight.reshape(up_weight.shape[0], 2, -1), (1, 0, 2)))
+    inward = pick(conv1_weight.T.reshape(2, part, -1)).reshape(part * 9, width)
+    inward = lax.dot_general(
+        inward, embed_table, (((1,), (1,)), ((), ())), preferred_element_type=jnp.float32
+    ).astype(BF)
+    inward = jnp.pad(inward.reshape(part, 9 * symbols), ((0, 8 - part), (0, 0)))
+    outward = jnp.pad(pick(conv2_weight.T.reshape(2, part, -1)), ((0, 8 - part), (0, 0)))
+    both = jnp.concatenate([inward, outward], axis=1)
+    both, rising = gather_blocks([both, rising], True, 1)
+    both = both.reshape(2 * SIDE * SIDE * 8, -1)
+    inward = both[:, : 9 * symbols]
+    outward = both[:, 9 * symbols :]
 
     starting, bounds = frame_layout(durations[0], utt_lengths[0], utt_order[0])
     ending = starting + durations[0]
@@ -223,14 +233,14 @@
     head = lax.ppermute(phone_ids[0, :4], "tm", [(i + 1, i) for i in range(ends)])
     tail = lax.ppermute(phone_ids[0, -4:], "tm", [(i, i + 1) for i in range(ends)])
     ids = jnp.concatenate([tail, phone_ids[0], head])
-    symbols = embed_table.shape[0]
-    choose = (ids[:, None] == jnp.arange(symbols, dtype=jnp.int32)[None, :]).astype(BF)
-    widened = jnp.dot(choose, embed_table, preferred_element_type=jnp.float32).astype(BF)
+    table = jnp.arange(symbols, dtype=jnp.int32)[None, :]
+    chosen = (phone_ids[0][:, None] == table).astype(BF)
+    embedded = jnp.dot(chosen, embed_table, preferred_element_type=jnp.float32)
     center = phone_labels[4 : 4 + phone_count]
     columns = []
     for tap in range(9):
-        keep = (phone_labels[tap : tap + phone_count] == center)[:, None]
-        columns.append(jnp.where(keep, widened[tap : tap + phone_count], jnp.zeros((), BF)))
+        keep = phone_labels[tap : tap + phone_count] == center
+        columns.append((jnp.where(keep, ids[tap : tap + phone_count], -1)[:, None] == table).astype(BF))
     unfolded = jnp.concatenate(columns, axis=1)
     filters = jnp.maximum(
         lax.dot_general(
@@ -239,7 +249,7 @@
         0.0,
     ).astype(BF)
     conv_out = jnp.dot(filters, outward, preferred_element_type=jnp.float32)
-    resid = widened[4 : 4 + phone_count].astype(jnp.float32) + conv_out
+    resid = embedded + conv_out
     middle = jnp.mean(resid, axis=1, keepdims=True)
     spread = jnp.mean((resid - middle) ** 2, axis=1, keepdims=True)
     decoded = ((resid - middle) * lax.rsqrt(spread + EPS) * norm_gain[None, :]).astype(BF)
@@ -286,49 +296,64 @@
     unfolded = jnp.concatenate(columns, axis=2).reshape(groups * inner, -1)
     summed = jnp.dot(unfolded, pre_flat, preferred_element_type=jnp.float32)
     act = jnp.where(summed >= 0, summed, 0.1 * summed).astype(BF).reshape(groups, inner, channels)
-    now = act[:, 1 : 1 + piece].reshape(F_DEV, channels)
+    place = jnp.arange(channels, dtype=jnp.int32)
+    unit = place // (SIDE * 8) * 8 + place // 8 % SIDE * (SIDE * 8) + place % 8
+    turn = (place[:, None] == unit[None, :]).astype(BF)
+    turned = jnp.dot(
+        act.reshape(groups * inner, channels), turn, preferred_element_type=jnp.float32
+    ).astype(BF).reshape(groups, inner, channels)
     keep_prev = (mine[:, :piece] == mine[:, 1 : 1 + piece])[:, :, None]
     keep_next = (mine[:, 2:] == mine[:, 1 : 1 + piece])[:, :, None]
-    prev = jnp.where(keep_prev, act[:, :piece], jnp.zeros((), BF)).reshape(F_DEV, channels)
-    nxt = jnp.where(keep_next, act[:, 2:], jnp.zeros((), BF)).reshape(F_DEV, channels)
+
+    def windowed(cells, offset, keep=None):
+        cells = cells[:, offset : offset + piece]
+        if keep is not None:
+            cells = jnp.where(keep, cells, jnp.zeros((), BF))
+        return cells.reshape(F_DEV, channels)
 
     out_width = up_weight.shape[2]
-    early = jnp.transpose(rising[0], (2, 1, 0, 3, 4))
-    late = jnp.transpose(rising[1], (2, 0, 1, 3, 4))
-    early = early.reshape(8, channels, out_width)
-    late = late.reshape(8, channels, out_width)
-    upsampled = upsample(now, prev, nxt, early, late)
+    upsampled = upsample(
+        windowed(turned, 1),
+        windowed(act, 1),
+        windowed(act, 0, keep_prev),
+        windowed(turned, 2, keep_next),
+        rising.reshape(2, channels, -1),
+        out_width,
+    )
     return upsampled.reshape(1, 1, groups, -1, out_width)
 
 
-def upsample_kernel(now, prev, nxt, early, late, out, total):
+def upsample_kernel(early_now, late_now, prev, nxt, taps, out, total):
     f32 = jnp.float32
+    width = out.shape[2]
+
+    def tap(number):
+        return taps[number // 8, :, pl.ds(number % 8 * width, width)]
+
     for r in range(8):
         if r < 4:
-            value = jnp.dot(now[...], early[r + 4], preferred_element_type=f32)
-            value += jnp.dot(prev[...], late[r + 4], preferred_element_type=f32)
+            value = jnp.dot(early_now[...], tap(r + 4), preferred_element_type=f32)
+            value += jnp.dot(prev[...], tap(r + 12), preferred_element_type=f32)
         else:
-            value = jnp.dot(now[...], late[r - 4], preferred_element_type=f32)
-            value += jnp.dot(nxt[...], early[r - 4], preferred_element_type=f32)
+            value = jnp.dot(late_now[...], tap(r + 4), preferred_element_type=f32)
+            value += jnp.dot(nxt[...], tap(r - 4), preferred_element_type=f32)
         total[:, r, :] = value
     out[...] = total[...].astype(out.dtype)
 
 
-def upsample(now, prev, nxt, early, late):
-    frames, channels = now.shape
-    width = early.shape[2]
+def upsample(early_now, late_now, prev, nxt, taps, width):
+    frames, channels = prev.shape
     rows = 64
     tile = pl.BlockSpec((rows, channels), lambda i: (i, 0))
-    whole = pl.BlockSpec((8, channels, width), lambda i: (0, 0, 0))
     return pl.pallas_call(
         upsample_kernel,
         grid=(frames // rows,),
         out_shape=jax.ShapeDtypeStruct((frames, 8, width), BF),
-        in_specs=[tile, tile, tile, whole, whole],
+        in_specs=[tile, tile, tile, tile, pl.BlockSpec(taps.shape, lambda i: (0, 0, 0))],
         out_specs=pl.BlockSpec((rows, 8, width), lambda i: (i, 0, 0)),
         scratch_shapes=[pltpu.VMEM((rows, 8, width), jnp.float32)],
         name="upsample",
-    )(now, prev, nxt, early, late)
+    )(early_now, late_now, prev, nxt, taps)
 
 
 def solution(mesh):

time: 148 us -> 136 us (0.919)
  Pallas kernels: 99.1 us -> 82.2 us
  local copies, waits for them, and re-layouts: 13.6 us -> 7.16 us
  waiting for transfers between devices: 0.01 us -> 4.91 us
  starting transfers between devices: 11 us -> 14.7 us
  other arithmetic: 13.5 us -> 16.3 us
    pallas_call x2, Pallas kernels: 92.1 us -> 75.2 us  [gather_blocks(): pl.pallas_call(functools.partial(gather_kernel, count, share), out_shape=...]
    transpose x3 -> x0, local copies, waits for them, and re-layouts: 5.93 us -> none  [the longest x2 4.3 us: shards(): late = jnp.transpose(rising[1], (2, 0, 1, 3, 4))]
    all_to_all x1, waiting for transfers between devices: 0.01 us -> 4.91 us  [shards(): lax.all_to_all(windows.reshape(groups, span, WIDE), 'utt', split_axis=0,...]
    all_to_all x1, starting transfers between devices: 4.92 us -> 8.6 us  [shards(): lax.all_to_all(windows.reshape(groups, span, WIDE), 'utt', split_axis=0,...]
    unnamed x14 -> x15, other arithmetic: 2.83 us -> 3.51 us
  transfers between devices with their start and end apart: 3 -> 3, of which waited for: 0 -> 1; matrix products, arithmetic and copies ran while one was open for 15% -> 13% of each run, Pallas kernels for 44% -> 39%
where the time goes in v3:
time: 136 us; the launch traced here: 135 us
  Pallas kernels  82.2 us (60%)
  other arithmetic  16.3 us (12%)
  starting transfers between devices  14.7 us (11%)
  matrix products  9.52 us (7%)
  local copies, waits for them, and re-layouts  7.16 us (5%)
  waiting for transfers between devices  4.91 us (4%)
    pallas_call x2, Pallas kernels, gather_blocks(): pl.pallas_call(functools.partial(gather_kernel, count, share), out_shape=...  75.2 us
    all_to_all x1, starting transfers between devices, shards(): lax.all_to_all(windows.reshape(groups, span, WIDE), 'utt', split_axis=0,...  8.6 us
    pallas_call x1, Pallas kernels, upsample(): pl.pallas_call(upsample_kernel, grid=(frames // rows,), out_shape=jax.Sha...  7.03 us
    all_to_all x1, waiting for transfers between devices, shards(): lax.all_to_all(windows.reshape(groups, span, WIDE), 'utt', split_axis=0,...  4.91 us
    ppermute x1, starting transfers between devices, shards(): lax.ppermute(phone_ids[0, -4:], 'tm', [(i, i + 1) for i in range(ends)])  4.8 us
    dot_general x1, matrix products, shards(): conv_out = jnp.dot(filters, outward, preferred_element_type=jnp.float32)  4.36 us
    unnamed x15, other arithmetic  3.51 us
    dot_general x1, matrix products, shards(): jnp.dot(hit.astype(BF), portion, preferred_element_type=jnp.float32)  3.07 us
  transfers between devices with their start and end apart: 3, of which 1 were waited for; matrix products, arithmetic and copies ran while one was open for 13% of the time, Pallas kernels for 39%

profile of v3, /device:TPU:1, one launch (start us, length us, event | category | flops | bytes accessed | tf_op | source)
XLA Modules:
  0.0 135.1 jit_solution(10963178830213138780)
XLA Ops:
  0.0 0.8 slice_bitcast_fusion
  0.8 4.8 %collective-permute-start = (s32[4]{0:T(128)S(1)}, s32[4]{0:T(128)S(1)}, u32[]{:S(2)}, u32[]{:S(2)}) collective-permute-start(s32[4]{0:T(128)S(1)} %get-tuple-element.41), channel_id=1, source_target_pairs={{0,1},{1,2},{2,3},{3,4},{4,5},{5,6},{6,7},{7,8},{8,9},{9,10},{10,1... | collective-permute-start | bytes 56 | tf_op jit(solution)/shard_map/ppermute | solution.py:234
  5.6 1.3 collective-permute-start.1
  6.9 0.7 copy.43
  7.7 0.1 reduce-window.18
  7.8 0.1 reduce.2
  7.9 0.7 compare_select_fusion.1
  8.6 0.7 fusion.64
  9.2 1.0 reduce-window.11
  10.4 0.1 convert_reduce_fusion
  10.5 1.0 slice_select_fusion.9
  11.6 0.2 convolution_convert_fusion.1
  11.8 0.8 slice_select_fusion.11
  12.6 0.9 reshape.233
  13.5 0.6 fusion.48.refs_1_
  14.1 0.9 fusion.35
  15.0 0.1 slice_reduce_fusion
  15.2 0.8 fusion.68
  16.1 0.8 select_reduce_fusion.2
  16.9 0.8 gather_fusion.1
  17.6 0.8 gather_fusion
  18.4 0.2 select_reduce_fusion.1
  18.6 0.3 select_reduce_fusion
  19.1 0.5 broadcast.275
  19.6 1.4 %reduce.8 = s32[4096]{0:T(1024)S(1)} reduce(s32[1,4096]{1,0:T(1,128)} %param.15, s32[]{:T(128)} %broadcast.275), dimensions={0}, to_apply=%param.15.reduce_sub_computation.3 | reduce | bytes 32772 | tf_op args[1]
  21.4 0.8 select_reduce_fusion.3
  22.2 0.1 add.148
  22.3 0.6 fusion.47.refs_0_
  22.9 52.2 %gather1.1 = (bf16[2,8,8,8,2688]{4,3,2,1,0:T(8,128)(2,1)}, bf16[2,8,8,8,2048]{4,3,2,1,0:T(8,128)(2,1)}) custom-call(bf16[8,2688]{1,0:T(8,128)(2,1)} %fusion.47.refs_0_, bf16[8,2048]{1,0:T(8,128)(2,1)} %fusion.48.refs_1_), custom_call_target="tpu_custom_call" | custom-call | tf_op jit(solution)/shard_map/gather1/pallas_call | solution.py:148
  75.1 1.1 pad.19
  76.3 0.8 pad_add_fusion.1
  77.1 0.1 fusion.36
  77.2 0.1 fusion.37
  77.3 0.1 fusion.38
  77.4 0.1 fusion.39
  77.5 0.7 fusion.34
  78.3 0.1 fusion.40
  78.4 0.1 fusion.41
  78.5 0.1 fusion.42
  78.6 0.1 fusion.43
  78.7 4.4 %fusion.69 = (f32[64]{0:T(128)S(1)}, f32[64,384]{1,0:T(8,128)S(1)}) fusion(f32[64,384]{1,0:T(8,128)S(1)} %fusion.35, bf16[1024,2688]{1,0:T(8,128)(2,1)} %bitcast.74, pred[64,2304]{1,0:T(8,128)(4,1)S(1)} %fusion.43), kind=kOutput, calls=%fused_computation.157 | convolution fusion | flops 352501696 | bytes 5849344 | tf_op jit(solution)/shard_map/dot_general | solution.py:251
  83.1 0.2 multiply_reduce_fusion
  83.3 0.2 convolution_convert_fusion.2
  83.5 0.7 select_add_fusion.refs_0_
  84.2 23.0 %gather2.1 = bf16[1,8,8,64,128]{4,3,2,1,0:T(8,128)(2,1)} custom-call(bf16[64,128]{1,0:T(8,128)(2,1)} %select_add_fusion.refs_0_), custom_call_target="tpu_custom_call" | custom-call | tf_op jit(solution)/shard_map/gather2/pallas_call | solution.py:148
  107.2 3.1 %fusion.15 = bf16[320,128]{1,0:T(8,128)(2,1)} fusion(bf16[4096,128]{1,0:T(8,128)(2,1)} %bitcast.60, s32[4096]{0:T(1024)S(1)} %lt.51, s32[4096]{0:T(1024)S(1)} %ge.27, s32[320]{0:T(512)S(1)} %add.148), kind=kOutput, calls=%fused_computation.15 | convolution fusion | flops 339517440 | bytes 1164544 | tf_op jit(solution)/shard_map/dot_general | solution.py:282
  110.3 8.6 %all-to-all-start = ((bf16[8,40,128]{2,1,0:T(8,128)(2,1)}), bf16[8,40,128]{2,1,0:T(8,128)(2,1)S(1)}, u32[]{:S(2)}, u32[]{:S(2)}) async-start(bf16[8,40,128]{2,1,0:T(8,128)(2,1)} %bitcast.20), calls=%async_computation | async-start | bytes 163840 | tf_op jit(solution)/shard_map/all_to_all | solution.py:283
  118.9 4.9 %all-to-all-done = bf16[8,40,128]{2,1,0:T(8,128)(2,1)S(1)} async-done(((bf16[8,40,128]{2,1,0:T(8,128)(2,1)}), bf16[8,40,128]{2,1,0:T(8,128)(2,1)S(1)}, u32[]{:S(2)}, u32[]{:S(2)}) %all-to-all-start) | async-done | bytes 81952 | tf_op jit(solution)/shard_map/all_to_all | solution.py:283
  123.8 0.1 slice.237
  123.9 0.1 copy.48
  124.2 0.1 fusion.33
  124.3 0.1 fusion.32
  124.4 0.1 fusion.31
  124.6 0.1 fusion.30
  124.7 0.1 fusion.29
  124.8 0.1 fusion.28
  125.0 0.1 fusion.27
  125.1 0.1 reshape.237
  125.3 0.5 fusion.22
  125.8 0.4 convolution_convert_fusion
  126.2 0.1 reshape.239
  126.3 0.9 slice_select_fusion.1
  127.2 0.9 slice_select_fusion
  128.1 7.0 %upsample.1 = bf16[256,8,256]{2,1,0:T(8,128)(2,1)} custom-call(bf16[256,512]{1,0:T(8,128)(2,1)} %bitcast.59, bf16[256,512]{1,0:T(8,128)(2,1)} %bitcast.57, bf16[256,512]{1,0:T(8,128)(2,1)} %bitcast.56, bf16[256,512]{1,0:T(8,128)(2,1)} %bitcast.58, bf16[2,512,2048]{2,1,0:T(8,128)(2,1)} %bitcast.55), custom_call_target="tpu_custom_call" | custom-call | tf_op jit(solution)/shard_map/upsample/pallas_call | solution.py:348
  (41 shorter events, 1.5 us)
Async XLA Ops:
  0.0 11.6 %copy-start = (bf16[256,384]{1,0:T(8,128)(2,1)S(1)}, bf16[256,384]{1,0:T(8,128)(2,1)}, u32[]{:S(2)}) copy-start(bf16[256,384]{1,0:T(8,128)(2,1)} %param.19) | copy-start | bytes 589828
  0.8 75.4 %collective-permute-start = (s32[4]{0:T(128)S(1)}, s32[4]{0:T(128)S(1)}, u32[]{:S(2)}, u32[]{:S(2)}) collective-permute-start(s32[4]{0:T(128)S(1)} %get-tuple-element.41), channel_id=1, source_target_pairs={{0,1},{1,2},{2,3},{3,4},{4,5},{5,6},{6,7},{7,8},{8,9},{9,10},{10,1... | collective-permute-start | bytes 56 | tf_op jit(solution)/shard_map/ppermute | solution.py:234
  5.6 70.6 %collective-permute-start.1 = (s32[4]{0:T(128)S(1)}, s32[4]{0:T(128)S(1)}, u32[]{:S(2)}, u32[]{:S(2)}) collective-permute-start(s32[4]{0:T(128)S(1)} %get-tuple-element.40), channel_id=1, source_target_pairs={{1,0},{2,1},{3,2},{4,3},{5,4},{6,5},{7,6},{8,7},{9,8},{10,9},{11,1... | collective-permute-start | bytes 56 | tf_op jit(solution)/shard_map/ppermute | solution.py:233
  16.0 67.2 %copy-start.1 = (bf16[384,80]{0,1:T(8,128)(2,1)S(1)}, bf16[384,80]{0,1:T(8,128)(2,1)}, u32[]{:S(2)}) copy-start(bf16[384,80]{0,1:T(8,128)(2,1)} %param.23) | copy-start | bytes 184324
  16.0 67.2 %copy-start.2 = (f32[384]{0:T(512)S(1)}, f32[384]{0:T(512)}, u32[]{:S(2)}) copy-start(f32[384]{0:T(512)} %param.22) | copy-start | bytes 4612
  110.3 13.5 %all-to-all-start = ((bf16[8,40,128]{2,1,0:T(8,128)(2,1)}), bf16[8,40,128]{2,1,0:T(8,128)(2,1)S(1)}, u32[]{:S(2)}, u32[]{:S(2)}) async-start(bf16[8,40,128]{2,1,0:T(8,128)(2,1)} %bitcast.20), calls=%async_computation | async-start | bytes 163840 | tf_op jit(solution)/shard_map/all_to_all | solution.py:283

commit v4 on v3

--- a/solution.py
+++ b/solution.py
@@ -19,10 +19,12 @@
 ORDER = (0, 1, 7, 2, 6, 3, 5, 4)
 
 
-def gather_kernel(count, share, *refs):
+def gather_kernel(count, share, near, *refs):
     blocks = refs[:count]
-    outs = refs[count : 2 * count]
-    local_sem, first_send, first_recv, ring_send, ring_recv, pair_send, pair_recv = refs[2 * count :]
+    outs = refs[count + near : 2 * count + near]
+    scratch = refs[2 * (count + near) :]
+    local_sem, first_send, first_recv, ring_send, ring_recv, pair_send, pair_recv = scratch[:7]
+    total = SIDE * SIDE
     utt = lax.axis_index("utt")
     tm = lax.axis_index("tm")
     core = lax.rem(utt, 2)
@@ -55,8 +57,26 @@
         )
     if share:
         pl.semaphore_signal(barrier, inc=1, device_id=(pair, tm), device_id_type=MESH)
-    pl.semaphore_wait(barrier, SIDE + 1 + (1 if share else 0))
-
+    if near:
+        for side in (1, total - 1):
+            pl.semaphore_signal(
+                barrier, inc=1, device_id=(utt, lax.rem(tm + side, total)), device_id_type=MESH
+            )
+    pl.semaphore_wait(barrier, SIDE + 1 + (1 if share else 0) + 2 * near)
+
+    beside_copies = []
+    if near:
+        for spot, side in ((0, 1), (1, total - 1)):
+            copy = pltpu.make_async_remote_copy(
+                src_ref=refs[count],
+                dst_ref=refs[2 * count + 1].at[spot],
+                send_sem=scratch[7].at[spot],
+                recv_sem=scratch[8].at[spot],
+                device_id=(utt, lax.rem(tm + side, total)),
+                device_id_type=MESH,
+            )
+            copy.start()
+            beside_copies.append(copy)
     own = [
         pltpu.make_async_copy(blocks[i], outs[i].at[half, second, first], local_sem.at[i])
         for i in range(count)
@@ -77,7 +97,7 @@
         block = lax.rem(first - order + SIDE, SIDE)
         spot = outs[i].at[half, beside(-side * step), block]
         return pltpu.make_async_remote_copy(
-            src_ref=spot,
+            src_ref=blocks[i] if step == 0 and order == 0 else spot,
             dst_ref=spot,
             send_sem=ring_send.at[i, way, step, order],
             recv_sem=ring_recv.at[i, way, step, order],
@@ -104,14 +124,14 @@
     for step in ORDER[1:]:
         for i in range(count):
             first_copy(i, step).start()
-    for copy in own:
-        copy.wait()
     for order in ORDER:
         for i in range(count):
             if order > 0:
                 first_copy(i, order).wait_recv()
             for way in range(2):
                 ring_copy(i, way, 0, order).start()
+    for copy in own:
+        copy.wait()
     if share:
         for i in range(count):
             pair_copy(i, 0).start()
@@ -139,31 +159,88 @@
         for i in range(count):
             for step in range(-3, 5):
                 pair_copy(i, step).wait()
-
-
-def gather_blocks(blocks, share, number):
+    for copy in beside_copies:
+        copy.wait()
+
+
+def gather_blocks(blocks, share, number, beside=None):
     count = len(blocks)
+    near = 0 if beside is None else 1
     halves = 2 if share else 1
     ring = (count, 2, SIDE // 2, SIDE)
+    shapes = [
+        jax.ShapeDtypeStruct((halves, SIDE, SIDE) + block.shape, block.dtype) for block in blocks
+    ]
+    scratch = [
+        pltpu.SemaphoreType.DMA((count,)),
+        pltpu.SemaphoreType.DMA((count, SIDE)),
+        pltpu.SemaphoreType.DMA((count, SIDE)),
+        pltpu.SemaphoreType.DMA(ring),
+        pltpu.SemaphoreType.DMA(ring),
+        pltpu.SemaphoreType.DMA((count, SIDE)),
+        pltpu.SemaphoreType.DMA((count, SIDE)),
+    ]
+    operands = list(blocks)
+    if near:
+        operands.append(beside)
+        shapes.append(jax.ShapeDtypeStruct((2,) + beside.shape, beside.dtype))
+        scratch += [pltpu.SemaphoreType.DMA((2,)), pltpu.SemaphoreType.DMA((2,))]
     return pl.pallas_call(
-        functools.partial(gather_kernel, count, share),
-        out_shape=[
-            jax.ShapeDtypeStruct((halves, SIDE, SIDE) + block.shape, block.dtype) for block in blocks
-        ],
-        in_specs=[pl.BlockSpec(memory_space=pl.ANY)] * count,
-        out_specs=[pl.BlockSpec(memory_space=pl.ANY)] * count,
+        functools.partial(gather_kernel, count, share, near),
+        out_shape=shapes,
+        in_specs=[pl.BlockSpec(memory_space=pl.ANY)] * (count + near),
+        out_specs=[pl.BlockSpec(memory_space=pl.ANY)] * (count + near),
+        scratch_shapes=scratch,
+        compiler_params=pltpu.CompilerParams(collective_id=number, has_side_effects=True),
+        name=f"gather{number}",
+    )(*operands)
+
+
+def exchange_kernel(given, taken, local_sem, send_sem, recv_sem):
+    utt = lax.axis_index("utt")
+    tm = lax.axis_index("tm")
+    groups = given.shape[0]
+    barrier = pltpu.get_barrier_semaphore()
+    for step in range(1, groups):
+        pl.semaphore_signal(
+            barrier, inc=1, device_id=(lax.rem(utt + step, groups), tm), device_id_type=MESH
+        )
+    pl.semaphore_wait(barrier, groups - 1)
+    own = pltpu.make_async_copy(given.at[utt], taken.at[utt], local_sem)
+    copies = []
+    for step in range(1, groups):
+        other = lax.rem(utt + step, groups)
+        copy = pltpu.make_async_remote_copy(
+            src_ref=given.at[other],
+            dst_ref=taken.at[utt],
+            send_sem=send_sem.at[step],
+            recv_sem=recv_sem.at[step],
+            device_id=(other, tm),
+            device_id_type=MESH,
+        )
+        copy.start()
+        copies.append(copy)
+    own.start()
+    own.wait()
+    for copy in copies:
+        copy.wait()
+
+
+def exchange(windows, number):
+    groups = windows.shape[0]
+    return pl.pallas_call(
+        exchange_kernel,
+        out_shape=jax.ShapeDtypeStruct(windows.shape, windows.dtype),
+        in_specs=[pl.BlockSpec(memory_space=pltpu.VMEM)],
+        out_specs=pl.BlockSpec(memory_space=pltpu.VMEM),
         scratch_shapes=[
-            pltpu.SemaphoreType.DMA((count,)),
-            pltpu.SemaphoreType.DMA((count, SIDE)),
-            pltpu.SemaphoreType.DMA((count, SIDE)),
-            pltpu.SemaphoreType.DMA(ring),
-            pltpu.SemaphoreType.DMA(ring),
-            pltpu.SemaphoreType.DMA((count, SIDE)),
-            pltpu.SemaphoreType.DMA((count, SIDE)),
+            pltpu.SemaphoreType.DMA,
+            pltpu.SemaphoreType.DMA((groups,)),
+            pltpu.SemaphoreType.DMA((groups,)),
         ],
         compiler_params=pltpu.CompilerParams(collective_id=number, has_side_effects=True),
-        name=f"gather{number}",
-    )(*blocks)
+        name="exchange",
+    )(windows)
 
 
 def utterance_of(indices, bounds):
@@ -207,7 +284,6 @@
     width = embed_table.shape[1]
     device = lax.axis_index("tm")
     core = lax.rem(lax.axis_index("utt"), 2)
-    ends = lax.axis_size("tm") - 1
 
     symbols = embed_table.shape[0]
     filters_here = conv1_weight.shape[1]
@@ -221,7 +297,7 @@
     inward = jnp.pad(inward.reshape(part, 9 * symbols), ((0, 8 - part), (0, 0)))
     outward = jnp.pad(pick(conv2_weight.T.reshape(2, part, -1)), ((0, 8 - part), (0, 0)))
     both = jnp.concatenate([inward, outward], axis=1)
-    both, rising = gather_blocks([both, rising], True, 1)
+    both, rising, aside = gather_blocks([both, rising], True, 1, phone_ids)
     both = both.reshape(2 * SIDE * SIDE * 8, -1)
     inward = both[:, : 9 * symbols]
     outward = both[:, 9 * symbols :]
@@ -230,9 +306,7 @@
     ending = starting + durations[0]
     nearby = device * phone_count + jnp.arange(-4, phone_count + 4, dtype=jnp.int32)
     phone_labels = jnp.where(nearby < 0, -1, utterance_of(nearby, bounds))
-    head = lax.ppermute(phone_ids[0, :4], "tm", [(i + 1, i) for i in range(ends)])
-    tail = lax.ppermute(phone_ids[0, -4:], "tm", [(i, i + 1) for i in range(ends)])
-    ids = jnp.concatenate([tail, phone_ids[0], head])
+    ids = jnp.concatenate([aside[0, 0, -4:], phone_ids[0], aside[1, 0, :4]])
     table = jnp.arange(symbols, dtype=jnp.int32)[None, :]
     chosen = (phone_ids[0][:, None] == table).astype(BF)
     embedded = jnp.dot(chosen, embed_table, preferred_element_type=jnp.float32)
@@ -280,9 +354,7 @@
         frames[:, None] < arranged(ending)[None, :]
     )
     windows = jnp.dot(hit.astype(BF), portion, preferred_element_type=jnp.float32).astype(BF)
-    arrived = lax.all_to_all(
-        windows.reshape(groups, span, WIDE), "utt", split_axis=0, concat_axis=0, tiled=True
-    )
+    arrived = exchange(windows.reshape(groups, span, WIDE), 3)
 
     labels = arrived[:, :, mel_width]
     channels = pre_weight.shape[2]

time: 136 us -> 130 us (0.956)
  starting transfers between devices: 14.7 us -> 0 us
  Pallas kernels: 82.2 us -> 94.2 us
  waiting for transfers between devices: 4.91 us -> 0 us
  other arithmetic: 16.3 us -> 17.7 us
    pallas_call x2 -> x3, Pallas kernels: 75.2 us -> 87.1 us  [the longest x2 74.7 us: gather_blocks(): pl.pallas_call(functools.partial(gather_kernel, count, share, near), out_...]
    all_to_all x1 -> x0, starting transfers between devices: 8.6 us -> none  [shards(): lax.all_to_all(windows.reshape(groups, span, WIDE), 'utt', split_axis=0,...]
    ppermute x2 -> x0, starting transfers between devices: 6.09 us -> none  [the longest x1 4.8 us: shards(): lax.ppermute(phone_ids[0, -4:], 'tm', [(i, i + 1) for i in range(ends)])]
    all_to_all x1 -> x0, waiting for transfers between devices: 4.91 us -> none  [shards(): lax.all_to_all(windows.reshape(groups, span, WIDE), 'utt', split_axis=0,...]
    unnamed x15, other arithmetic: 3.51 us -> 8.1 us
  transfers between devices with their start and end apart: 3 -> 0, of which waited for: 1 -> 0; matrix products, arithmetic and copies ran while one was open for 13% -> 0% of each run, Pallas kernels for 39% -> 0%
where the time goes in v4:
time: 130 us; the launch traced here: 129 us
  Pallas kernels  94.2 us (72%)
  other arithmetic  17.7 us (14%)
  matrix products  9.6 us (7%)
  local copies, waits for them, and re-layouts  6.88 us (5%)
    pallas_call x2, Pallas kernels, gather_blocks(): pl.pallas_call(functools.partial(gather_kernel, count, share, near), out_...  74.7 us
    pallas_call x1, Pallas kernels, exchange(): pl.pallas_call(exchange_kernel, out_shape=jax.ShapeDtypeStruct(windows.sh...  12.4 us
    unnamed x15, other arithmetic  8.1 us
    pallas_call x1, Pallas kernels, upsample(): pl.pallas_call(upsample_kernel, grid=(frames // rows,), out_shape=jax.Sha...  7.03 us
    dot_general x1, matrix products, shards(): conv_out = jnp.dot(filters, outward, preferred_element_type=jnp.float32)  4.36 us
    dot_general x1, matrix products, shards(): jnp.dot(hit.astype(BF), portion, preferred_element_type=jnp.float32)  3.13 us

profile of v4, /device:TPU:1, one launch (start us, length us, event | category | flops | bytes accessed | tf_op | source)
XLA Modules:
  0.0 128.7 jit_solution(9612328026525350300)
XLA Ops:
  0.0 1.0 slice_select_fusion.2
  1.1 0.2 convolution_convert_fusion.1
  1.4 0.8 slice_select_fusion.4
  2.2 0.6 fusion.40.refs_0_
  2.8 0.9 reshape.233
  3.7 0.6 fusion.41.refs_1_
  4.3 53.1 %gather1.1 = (bf16[2,8,8,8,2688]{4,3,2,1,0:T(8,128)(2,1)}, bf16[2,8,8,8,2048]{4,3,2,1,0:T(8,128)(2,1)}, s32[2,1,64]{2,1,0:T(1,128)}) custom-call(bf16[8,2688]{1,0:T(8,128)(2,1)} %fusion.40.refs_0_, bf16[8,2048]{1,0:T(8,128)(2,1)} %fusion.41.refs_1_, s32[1,64]{1,0:T(1,128)} %refs_2_.1), custom_call_target="tpu_custom_call" | custom-call | tf_op jit(solution)/shard_map/gather1/pallas_call | solution.py:188
  57.5 0.7 slice_bitcast_fusion
  58.2 0.8 pad_add_fusion.1
  59.0 0.7 copy.26
  59.7 0.1 reduce-window.18
  59.8 0.1 reduce.2
  59.9 0.1 convert_reduce_fusion
  60.0 0.1 compare_select_fusion.7
  60.1 0.1 fusion.29
  60.2 0.1 fusion.30
  60.3 0.1 fusion.31
  60.4 0.1 fusion.32
  60.5 0.7 fusion.27
  61.2 0.1 compare_select_fusion.3
  61.3 0.1 fusion.33
  61.4 0.1 fusion.34
  61.5 0.1 fusion.35
  61.6 0.1 fusion.36
  61.7 0.9 fusion.28
  62.5 4.4 %fusion.62 = (f32[64]{0:T(128)S(1)}, f32[64,384]{1,0:T(8,128)S(1)}) fusion(f32[64,384]{1,0:T(8,128)S(1)} %fusion.28, bf16[1024,2688]{1,0:T(8,128)(2,1)} %bitcast.72, pred[64,2304]{1,0:T(8,128)(4,1)S(1)} %fusion.36), kind=kOutput, calls=%fused_computation.151 | convolution fusion | flops 352501696 | bytes 5849344 | tf_op jit(solution)/shard_map/dot_general | solution.py:325
  66.9 0.2 multiply_reduce_fusion
  67.1 0.2 convolution_convert_fusion.2
  67.4 0.7 select_add_fusion.refs_0_
  68.0 21.6 %gather2.1 = bf16[1,8,8,64,128]{4,3,2,1,0:T(8,128)(2,1)} custom-call(bf16[64,128]{1,0:T(8,128)(2,1)} %select_add_fusion.refs_0_), custom_call_target="tpu_custom_call" | custom-call | tf_op jit(solution)/shard_map/gather2/pallas_call | solution.py:188
  89.7 0.3 reduce-window.11
  90.0 0.1 slice.227
  90.1 0.1 slice_reduce_fusion.1
  90.3 0.8 gather_fusion.1
  91.1 0.8 gather_fusion
  91.9 0.1 select_reduce_fusion.2
  92.0 0.2 select_reduce_fusion.1
  92.2 0.3 select_reduce_fusion
  92.6 0.1 reshape.227
  92.7 0.1 copy.24
  92.9 0.5 broadcast.276
  93.4 0.7 reduce.10
  94.2 0.1 fusion.60
  94.4 0.1 select_reduce_fusion.3
  94.6 0.1 add.148
  94.7 3.1 %fusion.15 = bf16[320,128]{1,0:T(8,128)(2,1)} fusion(bf16[4096,128]{1,0:T(8,128)(2,1)} %bitcast.59, s32[4096]{0:T(1024)S(1)} %lt.51, s32[4096]{0:T(1024)S(1)} %ge.27, s32[320]{0:T(512)S(1)} %add.148), kind=kOutput, calls=%fused_computation.15 | convolution fusion | flops 339517440 | bytes 1164544 | tf_op jit(solution)/shard_map/dot_general | solution.py:356
  97.8 12.4 %exchange.1 = bf16[8,40,128]{2,1,0:T(8,128)(2,1)} custom-call(bf16[8,40,128]{2,1,0:T(8,128)(2,1)} %bitcast.65), custom_call_target="tpu_custom_call" | custom-call | tf_op jit(solution)/shard_map/exchange/pallas_call | solution.py:231
  110.2 1.1 slice_reduce_fusion
  111.3 0.1 slice_compare_fusion.2
  111.4 1.0 select_dynamic-update-slice_fusion.6
  112.4 1.0 select_dynamic-update-slice_fusion.5
  113.4 1.0 select_dynamic-update-slice_fusion.4
  114.4 1.0 select_dynamic-update-slice_fusion.3
  115.5 1.0 select_dynamic-update-slice_fusion.2
  116.5 1.0 select_dynamic-update-slice_fusion.1
  117.5 1.0 select_dynamic-update-slice_fusion
  118.5 0.1 reshape.237
  118.8 0.5 fusion.22
  119.2 0.1 reshape.241
  119.4 0.9 slice_select_fusion.1
  120.3 0.4 convolution_convert_fusion
  120.7 0.1 reshape.239
  120.8 0.9 slice_select_fusion
  121.7 7.0 %upsample.1 = bf16[256,8,256]{2,1,0:T(8,128)(2,1)} custom-call(bf16[256,512]{1,0:T(8,128)(2,1)} %bitcast.58, bf16[256,512]{1,0:T(8,128)(2,1)} %bitcast.56, bf16[256,512]{1,0:T(8,128)(2,1)} %bitcast.55, bf16[256,512]{1,0:T(8,128)(2,1)} %bitcast.57, bf16[2,512,2048]{2,1,0:T(8,128)(2,1)} %bitcast.54), custom_call_target="tpu_custom_call" | custom-call | tf_op jit(solution)/shard_map/upsample/pallas_call | solution.py:420
  (45 shorter events, 1.1 us)
Async XLA Ops:
  0.0 1.1 copy-start
  0.0 89.7 %copy-start.5 = (s32[1,64]{1,0:T(1,128)S(1)}, s32[1,64]{1,0:T(1,128)}, u32[]{:S(2)}) copy-start(s32[1,64]{1,0:T(1,128)} %param.16) | copy-start | bytes 772
  0.0 67.1 %copy-start.4 = (f32[384]{0:T(512)S(1)}, f32[384]{0:T(512)}, u32[]{:S(2)}) copy-start(f32[384]{0:T(512)} %param.22) | copy-start | bytes 4612
  0.0 67.1 %copy-start.3 = (bf16[384,80]{0,1:T(8,128)(2,1)S(1)}, bf16[384,80]{0,1:T(8,128)(2,1)}, u32[]{:S(2)}) copy-start(bf16[384,80]{0,1:T(8,128)(2,1)} %param.23) | copy-start | bytes 184324
  0.0 89.7 %copy-start.2 = (s32[1,4096]{1,0:T(1,128)S(1)}, s32[1,4096]{1,0:T(1,128)}, u32[]{:S(2)}) copy-start(s32[1,4096]{1,0:T(1,128)} %param.15) | copy-start | bytes 49156
  3.7 88.2 %copy-start.6 = (s32[1,64]{1,0:T(1,128)S(1)}, s32[1,64]{1,0:T(1,128)}, u32[]{:S(2)}) copy-start(s32[1,64]{1,0:T(1,128)} %param.17) | copy-start | bytes 772
  61.5 32.9 %copy-start.7 = (s32[1,1,8]{2,1,0:T(1,128)S(1)}, s32[1,1,8]{2,1,0:T(1,128)}, u32[]{:S(2)}) copy-start(s32[1,1,8]{2,1,0:T(1,128)} %param.18) | copy-start | bytes 100
  94.7 24.0 %copy-start.1 = (bf16[7,80,512]{2,1,0:T(8,128)(2,1)S(1)}, bf16[7,80,512]{2,1,0:T(8,128)(2,1)}, u32[]{:S(2)}) copy-start(bf16[7,80,512]{2,1,0:T(8,128)(2,1)} %param.24) | copy-start | bytes 1720324

commit v5 on v4

--- a/solution.py
+++ b/solution.py
@@ -356,76 +356,86 @@
     windows = jnp.dot(hit.astype(BF), portion, preferred_element_type=jnp.float32).astype(BF)
     arrived = exchange(windows.reshape(groups, span, WIDE), 3)
 
-    labels = arrived[:, :, mel_width]
+    out_width = up_weight.shape[2]
     channels = pre_weight.shape[2]
-    pre_flat = jnp.pad(pre_weight, ((0, 0), (0, WIDE - mel_width), (0, 0))).reshape(-1, channels)
-    inner = piece + 2
-    mine = labels[:, 3 : 3 + inner]
-    columns = []
-    for tap in range(7):
-        keep = (labels[:, tap : tap + inner] == mine)[:, :, None]
-        columns.append(jnp.where(keep, arrived[:, tap : tap + inner], jnp.zeros((), BF)))
-    unfolded = jnp.concatenate(columns, axis=2).reshape(groups * inner, -1)
-    summed = jnp.dot(unfolded, pre_flat, preferred_element_type=jnp.float32)
-    act = jnp.where(summed >= 0, summed, 0.1 * summed).astype(BF).reshape(groups, inner, channels)
-    place = jnp.arange(channels, dtype=jnp.int32)
-    unit = place // (SIDE * 8) * 8 + place // 8 % SIDE * (SIDE * 8) + place % 8
-    turn = (place[:, None] == unit[None, :]).astype(BF)
-    turned = jnp.dot(
-        act.reshape(groups * inner, channels), turn, preferred_element_type=jnp.float32
-    ).astype(BF).reshape(groups, inner, channels)
-    keep_prev = (mine[:, :piece] == mine[:, 1 : 1 + piece])[:, :, None]
-    keep_next = (mine[:, 2:] == mine[:, 1 : 1 + piece])[:, :, None]
-
-    def windowed(cells, offset, keep=None):
-        cells = cells[:, offset : offset + piece]
-        if keep is not None:
-            cells = jnp.where(keep, cells, jnp.zeros((), BF))
-        return cells.reshape(F_DEV, channels)
-
-    out_width = up_weight.shape[2]
-    upsampled = upsample(
-        windowed(turned, 1),
-        windowed(act, 1),
-        windowed(act, 0, keep_prev),
-        windowed(turned, 2, keep_next),
-        rising.reshape(2, channels, -1),
-        out_width,
+    upsampled = vocoder(
+        arrived.reshape(groups * span, WIDE), pre_weight, rising.reshape(2, channels, -1),
+        groups, piece, out_width,
     )
     return upsampled.reshape(1, 1, groups, -1, out_width)
 
 
-def upsample_kernel(early_now, late_now, prev, nxt, taps, out, total):
+def vocoder_kernel(groups, piece, cells_ref, pre, taps_ref, out, taps, total, sem):
     f32 = jnp.float32
+    fetch = pltpu.make_async_copy(taps_ref, taps, sem)
+    fetch.start()
+    cells = cells_ref[...].astype(f32)
+    rows = cells.shape[0]
+    mel_width, channels = pre.shape[1:]
     width = out.shape[2]
 
-    def tap(number):
+    def ahead(values, steps):
+        return values if steps == 0 else pltpu.roll(values, (rows - steps) % rows, 0)
+
+    label = cells[:, mel_width : mel_width + 1]
+    summed = jnp.zeros((rows, channels), f32)
+    for tap in range(7):
+        moved = ahead(cells, tap - 3)
+        keep = moved[:, mel_width : mel_width + 1] == label
+        kept = jnp.where(keep, moved, 0.0).astype(BF)
+        summed += jnp.dot(kept[:, :mel_width], pre[tap], preferred_element_type=f32)
+    act = jnp.where(summed >= 0, summed, 0.1 * summed).astype(BF)
+    row = lax.broadcasted_iota(jnp.int32, (channels, channels), 0)
+    place = lax.broadcasted_iota(jnp.int32, (channels, channels), 1)
+    unit = (place // 64) * 8 + ((place // 8) % 8) * 64 + place % 8
+    turn = jnp.where(row == unit, 1.0, 0.0).astype(BF)
+    turned = jnp.dot(act, turn, preferred_element_type=f32)
+    act = act.astype(f32)
+
+    def windowed(values, offset):
+        values = ahead(values, REACH + offset)
+        if offset != 0:
+            same = ahead(cells, REACH + offset) == ahead(cells, REACH)
+            keep = jnp.where(same, 1.0, 0.0)[:, mel_width : mel_width + 1]
+            values = jnp.where(keep > 0.5, values, 0.0)
+        values = values.reshape(groups, rows // groups, channels)[:, :piece]
+        return values.reshape(groups * piece, channels).astype(BF)
+
+    late_now = windowed(act, 0)
+    early_now = windowed(turned, 0)
+    prev = windowed(act, -1)
+    nxt = windowed(turned, 1)
+    fetch.wait()
+
+    def part(number):
         return taps[number // 8, :, pl.ds(number % 8 * width, width)]
 
     for r in range(8):
         if r < 4:
-            value = jnp.dot(early_now[...], tap(r + 4), preferred_element_type=f32)
-            value += jnp.dot(prev[...], tap(r + 12), preferred_element_type=f32)
+            value = jnp.dot(early_now, part(r + 4), preferred_element_type=f32)
+            value += jnp.dot(prev, part(r + 12), preferred_element_type=f32)
         else:
-            value = jnp.dot(late_now[...], tap(r + 4), preferred_element_type=f32)
-            value += jnp.dot(nxt[...], tap(r - 4), preferred_element_type=f32)
+            value = jnp.dot(late_now, part(r + 4), preferred_element_type=f32)
+            value += jnp.dot(nxt, part(r - 4), preferred_element_type=f32)
         total[:, r, :] = value
     out[...] = total[...].astype(out.dtype)
 
 
-def upsample(early_now, late_now, prev, nxt, taps, width):
-    frames, channels = prev.shape
-    rows = 64
-    tile = pl.BlockSpec((rows, channels), lambda i: (i, 0))
+def vocoder(cells, pre_weight, taps, groups, piece, width):
+    vmem = pl.BlockSpec(memory_space=pltpu.VMEM)
+    frames = groups * piece
     return pl.pallas_call(
-        upsample_kernel,
-        grid=(frames // rows,),
+        functools.partial(vocoder_kernel, groups, piece),
         out_shape=jax.ShapeDtypeStruct((frames, 8, width), BF),
-        in_specs=[tile, tile, tile, tile, pl.BlockSpec(taps.shape, lambda i: (0, 0, 0))],
-        out_specs=pl.BlockSpec((rows, 8, width), lambda i: (i, 0, 0)),
-        scratch_shapes=[pltpu.VMEM((rows, 8, width), jnp.float32)],
-        name="upsample",
-    )(early_now, late_now, prev, nxt, taps)
+        in_specs=[vmem, vmem, pl.BlockSpec(memory_space=pl.ANY)],
+        out_specs=vmem,
+        scratch_shapes=[
+            pltpu.VMEM(taps.shape, taps.dtype),
+            pltpu.VMEM((frames, 8, width), jnp.float32),
+            pltpu.SemaphoreType.DMA,
+        ],
+        name="vocoder",
+    )(cells, pre_weight, taps)
 
 
 def solution(mesh):

time: 130 us -> 117 us (0.900)
  other arithmetic: 17.7 us -> 8.61 us
  local copies, waits for them, and re-layouts: 6.88 us -> 5.43 us
    unnamed x15 -> x9, other arithmetic: 8.1 us -> 2.02 us
    select_n x2 -> x0, other arithmetic: 1.82 us -> none  [windowed(): cells = jnp.where(keep, cells, jnp.zeros((), BF))]
where the time goes in v5:
time: 117 us; the launch traced here: 116 us
  Pallas kernels  93.2 us (80%)
  matrix products  8.7 us (7%)
  other arithmetic  8.61 us (7%)
  local copies, waits for them, and re-layouts  5.43 us (5%)
    pallas_call x2, Pallas kernels, gather_blocks(): pl.pallas_call(functools.partial(gather_kernel, count, share, near), out_...  74.7 us
    pallas_call x1, Pallas kernels, exchange(): pl.pallas_call(exchange_kernel, out_shape=jax.ShapeDtypeStruct(windows.sh...  12.4 us
    pallas_call x1, Pallas kernels, vocoder(): pl.pallas_call(functools.partial(vocoder_kernel, groups, piece), out_shap...  6.12 us
    dot_general x1, matrix products, shards(): conv_out = jnp.dot(filters, outward, preferred_element_type=jnp.float32)  4.36 us
    dot_general x1, matrix products, shards(): jnp.dot(hit.astype(BF), portion, preferred_element_type=jnp.float32)  3.07 us
    select_n x3, other arithmetic, shards(): pick = lambda both: jnp.where(core == 0, both[0], both[1])  2.42 us

profile of v5, /device:TPU:1, one launch (start us, length us, event | category | flops | bytes accessed | tf_op | source)
XLA Modules:
  0.0 116.3 jit_solution(8103225773122055702)
XLA Ops:
  0.0 1.0 slice_select_fusion
  1.1 0.1 select_n.108
  1.1 0.0 copy-done
  1.1 0.2 convolution_convert_fusion
  1.3 0.1 reshape.159
  1.4 0.8 slice_select_fusion.2
  2.2 0.6 fusion.38.refs_0_
  2.8 0.9 reshape.160
  3.7 0.0 copy-start.5
  3.7 0.6 fusion.39.refs_1_
  4.3 53.1 %gather1.1 = (bf16[2,8,8,8,2688]{4,3,2,1,0:T(8,128)(2,1)}, bf16[2,8,8,8,2048]{4,3,2,1,0:T(8,128)(2,1)}, s32[2,1,64]{2,1,0:T(1,128)}) custom-call(bf16[8,2688]{1,0:T(8,128)(2,1)} %fusion.38.refs_0_, bf16[8,2048]{1,0:T(8,128)(2,1)} %fusion.39.refs_1_, s32[1,64]{1,0:T(1,128)} %refs_2_.1), custom_call_target="tpu_custom_call" | custom-call | tf_op jit(solution)/shard_map/gather1/pallas_call | solution.py:188
  57.5 0.7 slice_bitcast_fusion
  58.2 0.8 pad_add_fusion.1
  59.0 0.7 copy.26
  59.7 0.1 reduce-window.18
  59.8 0.1 reduce.2
  59.9 0.1 convert_reduce_fusion
  60.0 0.1 compare_select_fusion.6
  60.1 0.1 fusion.27
  60.2 0.1 fusion.28
  60.3 0.1 fusion.29
  60.4 0.1 fusion.30
  60.5 0.7 fusion.25
  61.2 0.1 compare_select_fusion.2
  61.3 0.1 fusion.31
  61.4 0.1 fusion.32
  61.5 0.0 copy-start.6
  61.5 0.1 fusion.33
  61.6 0.1 fusion.34
  61.7 0.9 fusion.26
  62.5 4.4 %fusion.47 = (f32[64]{0:T(128)S(1)}, f32[64,384]{1,0:T(8,128)S(1)}) fusion(f32[64,384]{1,0:T(8,128)S(1)} %fusion.26, bf16[1024,2688]{1,0:T(8,128)(2,1)} %bitcast.61, pred[64,2304]{1,0:T(8,128)(4,1)S(1)} %fusion.34), kind=kOutput, calls=%fused_computation.104 | convolution fusion | flops 352501696 | bytes 5849344 | tf_op jit(solution)/shard_map/dot_general | solution.py:325
  66.9 0.2 multiply_reduce_fusion
  67.1 0.0 copy-done.3
  67.1 0.0 copy-done.2
  67.1 0.2 convolution_convert_fusion.1
  67.4 0.7 select_add_fusion.refs_0_
  68.0 21.6 %gather2.1 = bf16[1,8,8,64,128]{4,3,2,1,0:T(8,128)(2,1)} custom-call(bf16[64,128]{1,0:T(8,128)(2,1)} %select_add_fusion.refs_0_), custom_call_target="tpu_custom_call" | custom-call | tf_op jit(solution)/shard_map/gather2/pallas_call | solution.py:188
  89.7 0.3 reduce-window.11
  90.0 0.1 slice.134
  90.1 0.1 reduce-window.14
  90.1 0.1 slice_reduce_fusion
  90.3 0.1 fusion.46
  90.3 0.8 gather_fusion.1
  91.1 0.8 gather_fusion
  91.9 0.1 select_reduce_fusion.2
  92.0 0.2 select_reduce_fusion.1
  92.2 0.3 select_reduce_fusion
  92.5 0.1 reduce_sum.69
  92.6 0.1 reshape.154
  92.7 0.1 copy.24
  92.7 0.1 copy.25
  92.8 0.1 reshape.153
  92.9 0.5 broadcast.154
  93.4 0.7 reduce.8
  94.1 0.1 squeeze.10
  94.2 0.1 fusion.45
  94.3 0.1 ge.21
  94.4 0.1 lt.41
  94.4 0.1 select_reduce_fusion.3
  94.6 0.1 iota_add_fusion
  94.6 0.1 add.104
  94.7 3.1 %fusion.15 = bf16[320,128]{1,0:T(8,128)(2,1)} fusion(bf16[4096,128]{1,0:T(8,128)(2,1)} %bitcast.48, s32[4096]{0:T(1024)S(1)} %lt.41, s32[4096]{0:T(1024)S(1)} %ge.21, s32[320]{0:T(512)S(1)} %add.104), kind=kOutput, calls=%fused_computation.13 | convolution fusion | flops 339517440 | bytes 1164544 | tf_op jit(solution)/shard_map/dot_general | solution.py:356
  97.8 12.4 %exchange.1 = bf16[8,40,128]{2,1,0:T(8,128)(2,1)} custom-call(bf16[8,40,128]{2,1,0:T(8,128)(2,1)} %bitcast.54), custom_call_target="tpu_custom_call" | custom-call | tf_op jit(solution)/shard_map/exchange/pallas_call | solution.py:231
  110.2 6.1 %vocoder.1 = bf16[256,8,256]{2,1,0:T(8,128)(2,1)} custom-call(bf16[320,128]{1,0:T(8,128)(2,1)} %bitcast.49, bf16[7,80,512]{2,1,0:T(8,128)(2,1)} %pre.1, bf16[2,512,2048]{2,1,0:T(8,128)(2,1)} %bitcast.47), custom_call_target="tpu_custom_call" | custom-call | tf_op jit(solution)/shard_map/vocoder/pallas_call | solution.py:427
  (24 shorter events, 0.1 us)
Async XLA Ops:
  0.0 1.1 copy-start
  0.0 89.7 %copy-start.4 = (s32[1,64]{1,0:T(1,128)S(1)}, s32[1,64]{1,0:T(1,128)}, u32[]{:S(2)}) copy-start(s32[1,64]{1,0:T(1,128)} %param.16) | copy-start | bytes 772
  0.0 67.1 %copy-start.3 = (f32[384]{0:T(512)S(1)}, f32[384]{0:T(512)}, u32[]{:S(2)}) copy-start(f32[384]{0:T(512)} %param.22) | copy-start | bytes 4612
  0.0 67.1 %copy-start.2 = (bf16[384,80]{0,1:T(8,128)(2,1)S(1)}, bf16[384,80]{0,1:T(8,128)(2,1)}, u32[]{:S(2)}) copy-start(bf16[384,80]{0,1:T(8,128)(2,1)} %param.23) | copy-start | bytes 184324
  0.0 89.7 %copy-start.1 = (s32[1,4096]{1,0:T(1,128)S(1)}, s32[1,4096]{1,0:T(1,128)}, u32[]{:S(2)}) copy-start(s32[1,4096]{1,0:T(1,128)} %param.15) | copy-start | bytes 49156
  3.7 88.2 %copy-start.5 = (s32[1,64]{1,0:T(1,128)S(1)}, s32[1,64]{1,0:T(1,128)}, u32[]{:S(2)}) copy-start(s32[1,64]{1,0:T(1,128)} %param.17) | copy-start | bytes 772
  61.5 32.9 %copy-start.6 = (s32[1,1,8]{2,1,0:T(1,128)S(1)}, s32[1,1,8]{2,1,0:T(1,128)}, u32[]{:S(2)}) copy-start(s32[1,1,8]{2,1,0:T(1,128)} %param.18) | copy-start | bytes 100

commit v6 on v5

--- a/solution.py
+++ b/solution.py
@@ -43,14 +43,11 @@
 
     barrier = pltpu.get_barrier_semaphore()
 
-    def greet(step, carry):
+    for side in (1, SIDE - 1):
         pl.semaphore_signal(
             barrier, inc=1,
-            device_id=(utt, place(lax.rem(first + step, SIDE), second)), device_id_type=MESH,
-        )
-        return carry
-
-    lax.fori_loop(1, SIDE, greet, 0)
+            device_id=(utt, place(lax.rem(first + side, SIDE), second)), device_id_type=MESH,
+        )
     for side in (1, -1):
         pl.semaphore_signal(
             barrier, inc=1, device_id=(utt, place(first, beside(side))), device_id_type=MESH
@@ -62,7 +59,7 @@
             pl.semaphore_signal(
                 barrier, inc=1, device_id=(utt, lax.rem(tm + side, total)), device_id_type=MESH
             )
-    pl.semaphore_wait(barrier, SIDE + 1 + (1 if share else 0) + 2 * near)
+    pl.semaphore_wait(barrier, 4 + (1 if share else 0) + 2 * near)
 
     beside_copies = []
     if near:
@@ -82,13 +79,17 @@
         for i in range(count)
     ]
 
-    def first_copy(i, step):
+    def first_copy(i, order):
+        side = 1 if order <= SIDE // 2 else SIDE - 1
+        back = order - 1 if side == 1 else order + 1
+        block = lax.rem(first - back + 2 * SIDE, SIDE)
+        spot = outs[i].at[half, second, block]
         return pltpu.make_async_remote_copy(
-            src_ref=blocks[i],
-            dst_ref=outs[i].at[half, second, first],
-            send_sem=first_send.at[i, step],
-            recv_sem=first_recv.at[i, step],
-            device_id=(utt, place(lax.rem(first + step, SIDE), second)),
+            src_ref=blocks[i] if back % SIDE == 0 else spot,
+            dst_ref=spot,
+            send_sem=first_send.at[i, order],
+            recv_sem=first_recv.at[i, order],
+            device_id=(utt, place(lax.rem(first + side, SIDE), second)),
             device_id_type=MESH,
         )
 
@@ -121,13 +122,17 @@
 
     for copy in own:
         copy.start()
-    for step in ORDER[1:]:
-        for i in range(count):
-            first_copy(i, step).start()
+    for i in range(count):
+        for order in (1, SIDE - 1):
+            first_copy(i, order).start()
     for order in ORDER:
         for i in range(count):
             if order > 0:
                 first_copy(i, order).wait_recv()
+                if order < SIDE // 2:
+                    first_copy(i, order + 1).start()
+                elif order > SIDE // 2 + 1:
+                    first_copy(i, order - 1).start()
             for way in range(2):
                 ring_copy(i, way, 0, order).start()
     for copy in own:
@@ -255,8 +260,9 @@
     utt_first = bounds - lengths
     inclusive = jnp.cumsum(lasting)
     exclusive = inclusive - lasting
-    first_frame = jnp.take(exclusive, utt_first)
-    utt_frames = jnp.take(inclusive, bounds - 1) - first_frame
+    last_frame = jnp.take(inclusive, bounds - 1)
+    first_frame = jnp.pad(last_frame, (1, 0))[:utt_count]
+    utt_frames = last_frame - first_frame
     slots = jnp.arange(utt_count, dtype=jnp.int32)
     places = jnp.sum(jnp.where(ordering[None, :] == slots[:, None], slots[None, :], 0), axis=1)
     offsets = jnp.sum(jnp.where(places[None, :] < places[:, None], utt_frames[None, :], 0), axis=1)

time: 117 us -> 121 us (1.034)
  Pallas kernels: 93.2 us -> 98 us
    pallas_call x2, Pallas kernels: 74.7 us -> 77.2 us  [gather_blocks(): pl.pallas_call(functools.partial(gather_kernel, count, share, near), out_...]
    pallas_call x1, Pallas kernels: 12.4 us -> 14.7 us  [exchange(): pl.pallas_call(exchange_kernel, out_shape=jax.ShapeDtypeStruct(windows.sh...]
where the time goes in v6:
time: 121 us; the launch traced here: 120 us
  Pallas kernels  98 us (81%)
  other arithmetic  8.74 us (7%)
  matrix products  8.7 us (7%)
  local copies, waits for them, and re-layouts  4.66 us (4%)
    pallas_call x2, Pallas kernels, gather_blocks(): pl.pallas_call(functools.partial(gather_kernel, count, share, near), out_...  77.2 us
    pallas_call x1, Pallas kernels, exchange(): pl.pallas_call(exchange_kernel, out_shape=jax.ShapeDtypeStruct(windows.sh...  14.7 us
    pallas_call x1, Pallas kernels, vocoder(): pl.pallas_call(functools.partial(vocoder_kernel, groups, piece), out_shap...  6.12 us
    dot_general x1, matrix products, shards(): conv_out = jnp.dot(filters, outward, preferred_element_type=jnp.float32)  4.36 us
    dot_general x1, matrix products, shards(): jnp.dot(hit.astype(BF), portion, preferred_element_type=jnp.float32)  3.07 us

profile of v6, /device:TPU:1, one launch (start us, length us, event | category | flops | bytes accessed | tf_op | source)
XLA Modules:
  0.0 120.3 jit_solution(13191592204260755762)
XLA Ops:
  0.0 0.0 copy-start
  0.0 1.0 slice_select_fusion
  1.0 0.1 select_n.124
  1.1 0.0 copy-start.5
  1.1 0.0 copy-start.4
  1.1 0.2 convolution_convert_fusion
  1.3 0.1 reshape.177
  1.4 0.8 slice_select_fusion.2
  2.2 0.6 fusion.38.refs_0_
  2.8 0.9 reshape.178
  3.7 0.0 copy-start.6
  3.7 0.6 fusion.40.refs_1_
  4.3 55.0 %gather1.1 = (bf16[2,8,8,8,2688]{4,3,2,1,0:T(8,128)(2,1)}, bf16[2,8,8,8,2048]{4,3,2,1,0:T(8,128)(2,1)}, s32[2,1,64]{2,1,0:T(1,128)}) custom-call(bf16[8,2688]{1,0:T(8,128)(2,1)} %fusion.38.refs_0_, bf16[8,2048]{1,0:T(8,128)(2,1)} %fusion.40.refs_1_, s32[1,64]{1,0:T(1,128)} %refs_2_.1), custom_call_target="tpu_custom_call" | custom-call | tf_op jit(solution)/shard_map/gather1/pallas_call | solution.py:193
  59.3 0.7 slice_bitcast_fusion
  60.0 0.8 pad_add_fusion.1
  60.8 0.7 copy.26
  61.5 0.1 reduce-window.18
  61.6 0.1 fusion.39
  61.8 0.1 convert_reduce_fusion
  61.9 0.1 compare_select_fusion.6
  62.0 0.1 fusion.27
  62.1 0.1 fusion.28
  62.1 0.1 fusion.29
  62.2 0.1 fusion.30
  62.3 0.7 fusion.25
  63.1 0.1 compare_select_fusion.2
  63.1 0.1 fusion.31
  63.2 0.1 fusion.32
  63.3 0.1 fusion.33
  63.4 0.1 fusion.34
  63.5 0.9 fusion.26
  64.4 4.4 %fusion.47 = (f32[64]{0:T(128)S(1)}, f32[64,384]{1,0:T(8,128)S(1)}) fusion(f32[64,384]{1,0:T(8,128)S(1)} %fusion.26, bf16[1024,2688]{1,0:T(8,128)(2,1)} %bitcast.54, pred[64,2304]{1,0:T(8,128)(4,1)S(1)} %fusion.34), kind=kOutput, calls=%fused_computation.101 | convolution fusion | flops 352501696 | bytes 5849344 | tf_op jit(solution)/shard_map/dot_general | solution.py:331
  68.7 0.2 multiply_reduce_fusion
  69.0 0.2 convolution_convert_fusion.1
  69.2 0.7 select_add_fusion.refs_0_
  69.9 22.2 %gather2.1 = bf16[1,8,8,64,128]{4,3,2,1,0:T(8,128)(2,1)} custom-call(bf16[64,128]{1,0:T(8,128)(2,1)} %select_add_fusion.refs_0_), custom_call_target="tpu_custom_call" | custom-call | tf_op jit(solution)/shard_map/gather2/pallas_call | solution.py:193
  92.1 0.3 reduce-window.11
  92.4 0.1 slice.136
  92.5 0.1 reduce-window.14
  92.5 0.1 slice_reduce_fusion
  92.7 0.1 add_bitcast_fusion
  92.7 0.8 gather_fusion
  93.5 0.1 fusion.44
  93.6 0.1 select_reduce_fusion.2
  93.7 0.2 select_reduce_fusion.1
  93.9 0.1 fusion.43
  94.0 0.3 select_reduce_fusion
  94.3 0.1 reduce_sum.69
  94.3 0.1 reshape.172
  94.4 0.1 copy.24
  94.5 0.1 copy.25
  94.6 0.1 reshape.171
  94.7 0.5 broadcast.184
  95.2 0.7 reduce.10
  95.9 0.1 squeeze.6
  95.9 0.1 fusion.46
  96.0 0.1 ge.26
  96.1 0.1 lt.60
  96.2 0.1 select_reduce_fusion.3
  96.3 0.1 iota_add_fusion
  96.4 0.1 add.134
  96.5 3.1 %fusion.15 = bf16[320,128]{1,0:T(8,128)(2,1)} fusion(bf16[4096,128]{1,0:T(8,128)(2,1)} %bitcast.42, s32[4096]{0:T(1024)S(1)} %lt.60, s32[4096]{0:T(1024)S(1)} %ge.26, s32[320]{0:T(512)S(1)} %add.134), kind=kOutput, calls=%fused_computation.12 | convolution fusion | flops 339517440 | bytes 1164544 | tf_op jit(solution)/shard_map/dot_general | solution.py:362
  99.5 14.7 %exchange.1 = bf16[8,40,128]{2,1,0:T(8,128)(2,1)} custom-call(bf16[8,40,128]{2,1,0:T(8,128)(2,1)} %bitcast.46), custom_call_target="tpu_custom_call" | custom-call | tf_op jit(solution)/shard_map/exchange/pallas_call | solution.py:236
  114.2 6.1 %vocoder.1 = bf16[256,8,256]{2,1,0:T(8,128)(2,1)} custom-call(bf16[320,128]{1,0:T(8,128)(2,1)} %bitcast.43, bf16[7,80,512]{2,1,0:T(8,128)(2,1)} %pre.1, bf16[2,512,2048]{2,1,0:T(8,128)(2,1)} %bitcast.41), custom_call_target="tpu_custom_call" | custom-call | tf_op jit(solution)/shard_map/vocoder/pallas_call | solution.py:433
  (22 shorter events, 0.1 us)
Async XLA Ops:
  0.0 1.1 copy-start
  0.0 68.9 %copy-start.3 = (f32[384]{0:T(512)S(1)}, f32[384]{0:T(512)}, u32[]{:S(2)}) copy-start(f32[384]{0:T(512)} %param.20) | copy-start | bytes 4612
  0.0 68.9 %copy-start.2 = (bf16[384,80]{0,1:T(8,128)(2,1)S(1)}, bf16[384,80]{0,1:T(8,128)(2,1)}, u32[]{:S(2)}) copy-start(bf16[384,80]{0,1:T(8,128)(2,1)} %param.21) | copy-start | bytes 184324
  0.0 92.1 %copy-start.1 = (s32[1,4096]{1,0:T(1,128)S(1)}, s32[1,4096]{1,0:T(1,128)}, u32[]{:S(2)}) copy-start(s32[1,4096]{1,0:T(1,128)} %param.13) | copy-start | bytes 49156
  1.1 92.5 %copy-start.5 = (s32[1,64]{1,0:T(1,128)S(1)}, s32[1,64]{1,0:T(1,128)}, u32[]{:S(2)}) copy-start(s32[1,64]{1,0:T(1,128)} %param.15) | copy-start | bytes 772
  1.1 92.8 %copy-start.4 = (s32[1,64]{1,0:T(1,128)S(1)}, s32[1,64]{1,0:T(1,128)}, u32[]{:S(2)}) copy-start(s32[1,64]{1,0:T(1,128)} %param.14) | copy-start | bytes 772
  3.7 92.5 %copy-start.6 = (s32[1,1,8]{2,1,0:T(1,128)S(1)}, s32[1,1,8]{2,1,0:T(1,128)}, u32[]{:S(2)}) copy-start(s32[1,1,8]{2,1,0:T(1,128)} %param.16) | copy-start | bytes 100

commit v7 on v5

--- a/solution.py
+++ b/solution.py
@@ -163,7 +163,7 @@
         copy.wait()
 
 
-def gather_blocks(blocks, share, number, beside=None):
+def gather_blocks(blocks, share, number, space, beside=None):
     count = len(blocks)
     near = 0 if beside is None else 1
     halves = 2 if share else 1
@@ -188,8 +188,8 @@
     return pl.pallas_call(
         functools.partial(gather_kernel, count, share, near),
         out_shape=shapes,
-        in_specs=[pl.BlockSpec(memory_space=pl.ANY)] * (count + near),
-        out_specs=[pl.BlockSpec(memory_space=pl.ANY)] * (count + near),
+        in_specs=[pl.BlockSpec(memory_space=space)] * (count + near),
+        out_specs=[pl.BlockSpec(memory_space=space)] * (count + near),
         scratch_shapes=scratch,
         compiler_params=pltpu.CompilerParams(collective_id=number, has_side_effects=True),
         name=f"gather{number}",
@@ -255,8 +255,9 @@
     utt_first = bounds - lengths
     inclusive = jnp.cumsum(lasting)
     exclusive = inclusive - lasting
-    first_frame = jnp.take(exclusive, utt_first)
-    utt_frames = jnp.take(inclusive, bounds - 1) - first_frame
+    last_frame = jnp.take(inclusive, bounds - 1)
+    first_frame = jnp.pad(last_frame, (1, 0))[:utt_count]
+    utt_frames = last_frame - first_frame
     slots = jnp.arange(utt_count, dtype=jnp.int32)
     places = jnp.sum(jnp.where(ordering[None, :] == slots[:, None], slots[None, :], 0), axis=1)
     offsets = jnp.sum(jnp.where(places[None, :] < places[:, None], utt_frames[None, :], 0), axis=1)
@@ -297,7 +298,7 @@
     inward = jnp.pad(inward.reshape(part, 9 * symbols), ((0, 8 - part), (0, 0)))
     outward = jnp.pad(pick(conv2_weight.T.reshape(2, part, -1)), ((0, 8 - part), (0, 0)))
     both = jnp.concatenate([inward, outward], axis=1)
-    both, rising, aside = gather_blocks([both, rising], True, 1, phone_ids)
+    both, rising, aside = gather_blocks([both, rising], True, 1, pl.ANY, phone_ids)
     both = both.reshape(2 * SIDE * SIDE * 8, -1)
     inward = both[:, : 9 * symbols]
     outward = both[:, 9 * symbols :]
@@ -332,7 +333,7 @@
     lane = lax.broadcasted_iota(jnp.int32, (phone_count, WIDE), 1)
     told = jnp.where(lane == mel_width, (center + 1).astype(BF)[:, None], jnp.zeros((), BF))
     mel_block = jnp.pad(mel_ph, ((0, 0), (0, WIDE - mel_width))) + told
-    (portion,) = gather_blocks([mel_block], False, 2)
+    (portion,) = gather_blocks([mel_block], False, 2, pltpu.VMEM)
     portion = portion.reshape(-1, WIDE)
 
     def arranged(values):

time: 117 us -> 116 us (level)
  no operation moved by 1% of the time
where the time goes in v7:
time: 116 us
  Pallas kernels  93.3 us (80%)
  other arithmetic  8.74 us (8%)
  matrix products  8.7 us (7%)
  local copies, waits for them, and re-layouts  4.66 us (4%)
    pallas_call x2, Pallas kernels, gather_blocks(): pl.pallas_call(functools.partial(gather_kernel, count, share, near), out_...  75 us
    pallas_call x1, Pallas kernels, exchange(): pl.pallas_call(exchange_kernel, out_shape=jax.ShapeDtypeStruct(windows.sh...  12.2 us
    pallas_call x1, Pallas kernels, vocoder(): pl.pallas_call(functools.partial(vocoder_kernel, groups, piece), out_shap...  6.12 us
    dot_general x1, matrix products, shards(): conv_out = jnp.dot(filters, outward, preferred_element_type=jnp.float32)  4.36 us
    dot_general x1, matrix products, shards(): jnp.dot(hit.astype(BF), portion, preferred_element_type=jnp.float32)  3.07 us
    select_n x3, other arithmetic, shards(): pick = lambda both: jnp.where(core == 0, both[0], both[1])  2.4 us

profile of v7, /device:TPU:1, one launch (start us, length us, event | category | flops | bytes accessed | tf_op | source)
XLA Modules:
  0.0 115.6 jit_solution(6438442994800703134)
XLA Ops:
  0.0 1.0 slice_select_fusion
  1.0 0.1 select_n.124
  1.1 0.0 copy-start.5
  1.1 0.0 copy-start.4
  1.1 0.2 convolution_convert_fusion
  1.3 0.1 reshape.177
  1.4 0.8 slice_select_fusion.2
  2.2 0.6 fusion.38.refs_0_
  2.8 0.9 reshape.178
  3.7 0.0 copy-start.6
  3.7 0.6 fusion.40.refs_1_
  4.3 53.1 %gather1.1 = (bf16[2,8,8,8,2688]{4,3,2,1,0:T(8,128)(2,1)}, bf16[2,8,8,8,2048]{4,3,2,1,0:T(8,128)(2,1)}, s32[2,1,64]{2,1,0:T(1,128)}) custom-call(bf16[8,2688]{1,0:T(8,128)(2,1)} %fusion.38.refs_0_, bf16[8,2048]{1,0:T(8,128)(2,1)} %fusion.40.refs_1_, s32[1,64]{1,0:T(1,128)} %refs_2_.1), custom_call_target="tpu_custom_call" | custom-call | tf_op jit(solution)/shard_map/gather1/pallas_call | solution.py:188
  57.5 0.7 slice_bitcast_fusion
  58.2 0.8 pad_add_fusion.1
  59.0 0.7 copy.26
  59.7 0.1 reduce-window.18
  59.8 0.1 fusion.39
  59.9 0.1 convert_reduce_fusion
  60.0 0.1 compare_select_fusion.6
  60.1 0.1 fusion.27
  60.2 0.1 fusion.28
  60.3 0.1 fusion.29
  60.4 0.1 fusion.30
  60.5 0.7 fusion.25
  61.2 0.1 compare_select_fusion.2
  61.3 0.1 fusion.31
  61.4 0.1 fusion.32
  61.5 0.1 fusion.33
  61.6 0.1 fusion.34
  61.7 0.9 fusion.26
  62.5 4.4 %fusion.47 = (f32[64]{0:T(128)S(1)}, f32[64,384]{1,0:T(8,128)S(1)}) fusion(f32[64,384]{1,0:T(8,128)S(1)} %fusion.26, bf16[1024,2688]{1,0:T(8,128)(2,1)} %bitcast.54, pred[64,2304]{1,0:T(8,128)(4,1)S(1)} %fusion.34), kind=kOutput, calls=%fused_computation.101 | convolution fusion | flops 352501696 | bytes 5849344 | tf_op jit(solution)/shard_map/dot_general | solution.py:326
  66.9 0.2 multiply_reduce_fusion
  67.1 0.0 copy-done.3
  67.1 0.2 convolution_convert_fusion.1
  67.3 0.7 select_add_fusion.refs_0_
  68.0 21.8 %gather2.1 = bf16[1,8,8,64,128]{4,3,2,1,0:T(8,128)(2,1)} custom-call(bf16[64,128]{1,0:T(8,128)(2,1)} %select_add_fusion.refs_0_), custom_call_target="tpu_custom_call" | custom-call | tf_op jit(solution)/shard_map/gather2/pallas_call | solution.py:188
  89.9 0.3 reduce-window.11
  90.2 0.1 slice.136
  90.2 0.1 reduce-window.14
  90.3 0.1 slice_reduce_fusion
  90.4 0.1 add_bitcast_fusion
  90.5 0.8 gather_fusion
  91.3 0.1 fusion.44
  91.4 0.1 select_reduce_fusion.2
  91.5 0.2 select_reduce_fusion.1
  91.7 0.1 fusion.43
  91.8 0.3 select_reduce_fusion
  92.0 0.1 reduce_sum.69
  92.1 0.1 reshape.172
  92.2 0.1 copy.24
  92.3 0.1 copy.25
  92.4 0.1 reshape.171
  92.4 0.5 broadcast.184
  92.9 0.7 reduce.10
  93.6 0.1 squeeze.6
  93.7 0.1 fusion.46
  93.8 0.1 ge.26
  93.9 0.1 lt.60
  94.0 0.1 select_reduce_fusion.3
  94.1 0.1 iota_add_fusion
  94.2 0.1 add.134
  94.2 3.1 %fusion.15 = bf16[320,128]{1,0:T(8,128)(2,1)} fusion(bf16[4096,128]{1,0:T(8,128)(2,1)} %bitcast.42, s32[4096]{0:T(1024)S(1)} %lt.60, s32[4096]{0:T(1024)S(1)} %ge.26, s32[320]{0:T(512)S(1)} %add.134), kind=kOutput, calls=%fused_computation.12 | convolution fusion | flops 339517440 | bytes 1164544 | tf_op jit(solution)/shard_map/dot_general | solution.py:357
  97.3 12.2 %exchange.1 = bf16[8,40,128]{2,1,0:T(8,128)(2,1)} custom-call(bf16[8,40,128]{2,1,0:T(8,128)(2,1)} %bitcast.46), custom_call_target="tpu_custom_call" | custom-call | tf_op jit(solution)/shard_map/exchange/pallas_call | solution.py:231
  109.5 6.1 %vocoder.1 = bf16[256,8,256]{2,1,0:T(8,128)(2,1)} custom-call(bf16[320,128]{1,0:T(8,128)(2,1)} %bitcast.43, bf16[7,80,512]{2,1,0:T(8,128)(2,1)} %pre.1, bf16[2,512,2048]{2,1,0:T(8,128)(2,1)} %bitcast.41), custom_call_target="tpu_custom_call" | custom-call | tf_op jit(solution)/shard_map/vocoder/pallas_call | solution.py:428
  (22 shorter events, 0.1 us)
Async XLA Ops:
  0.0 1.1 copy-start
  0.0 67.1 %copy-start.3 = (f32[384]{0:T(512)S(1)}, f32[384]{0:T(512)}, u32[]{:S(2)}) copy-start(f32[384]{0:T(512)} %param.20) | copy-start | bytes 4612
  0.0 67.1 %copy-start.2 = (bf16[384,80]{0,1:T(8,128)(2,1)S(1)}, bf16[384,80]{0,1:T(8,128)(2,1)}, u32[]{:S(2)}) copy-start(bf16[384,80]{0,1:T(8,128)(2,1)} %param.21) | copy-start | bytes 184324
  0.0 89.9 %copy-start.1 = (s32[1,4096]{1,0:T(1,128)S(1)}, s32[1,4096]{1,0:T(1,128)}, u32[]{:S(2)}) copy-start(s32[1,4096]{1,0:T(1,128)} %param.13) | copy-start | bytes 49156
  1.1 90.3 %copy-start.5 = (s32[1,64]{1,0:T(1,128)S(1)}, s32[1,64]{1,0:T(1,128)}, u32[]{:S(2)}) copy-start(s32[1,64]{1,0:T(1,128)} %param.15) | copy-start | bytes 772
  1.1 90.6 %copy-start.4 = (s32[1,64]{1,0:T(1,128)S(1)}, s32[1,64]{1,0:T(1,128)}, u32[]{:S(2)}) copy-start(s32[1,64]{1,0:T(1,128)} %param.14) | copy-start | bytes 772
  3.7 90.3 %copy-start.6 = (s32[1,1,8]{2,1,0:T(1,128)S(1)}, s32[1,1,8]{2,1,0:T(1,128)}, u32[]{:S(2)}) copy-start(s32[1,1,8]{2,1,0:T(1,128)} %param.16) | copy-start | bytes 100

commit v8 on v7

--- a/solution.py
+++ b/solution.py
@@ -51,7 +51,8 @@
         return carry
 
     lax.fori_loop(1, SIDE, greet, 0)
-    for side in (1, -1):
+    leap = not share
+    for side in (1, -1, 2, -2) if leap else (1, -1):
         pl.semaphore_signal(
             barrier, inc=1, device_id=(utt, place(first, beside(side))), device_id_type=MESH
         )
@@ -62,7 +63,7 @@
             pl.semaphore_signal(
                 barrier, inc=1, device_id=(utt, lax.rem(tm + side, total)), device_id_type=MESH
             )
-    pl.semaphore_wait(barrier, SIDE + 1 + (1 if share else 0) + 2 * near)
+    pl.semaphore_wait(barrier, SIDE + (1 if share else 3) + (1 if share else 0) + 2 * near)
 
     beside_copies = []
     if near:
@@ -95,13 +96,14 @@
     def ring_copy(i, way, step, order):
         side = 1 - 2 * way
         block = lax.rem(first - order + SIDE, SIDE)
-        spot = outs[i].at[half, beside(-side * step), block]
+        held, places = ((0, 1), (0, 2), (2, 1), (2, 2))[step] if leap else (step, 1)
+        spot = outs[i].at[half, beside(-side * held), block]
         return pltpu.make_async_remote_copy(
-            src_ref=blocks[i] if step == 0 and order == 0 else spot,
+            src_ref=blocks[i] if held == 0 and order == 0 else spot,
             dst_ref=spot,
             send_sem=ring_send.at[i, way, step, order],
             recv_sem=ring_recv.at[i, way, step, order],
-            device_id=(utt, place(first, beside(side))),
+            device_id=(utt, place(first, beside(side * places))),
             device_id_type=MESH,
         )
 
@@ -129,20 +131,23 @@
             if order > 0:
                 first_copy(i, order).wait_recv()
             for way in range(2):
-                ring_copy(i, way, 0, order).start()
+                for step in (0, 1) if leap else (0,):
+                    ring_copy(i, way, step, order).start()
     for copy in own:
         copy.wait()
     if share:
         for i in range(count):
             pair_copy(i, 0).start()
-    for step in range(SIDE // 2):
+    after = {0: (), 1: (2, 3), 2: (), 3: ()} if leap else {0: (1,), 1: (2,), 2: (3,), 3: ()}
+    for step in (1, 0, 2, 3) if leap else (0, 1, 2, 3):
         for order in ORDER:
             for i in range(count):
                 for way in range(2):
                     if step < steps_of(way, order):
                         ring_copy(i, way, step, order).wait_recv()
-                        if step + 1 < steps_of(way, order):
-                            ring_copy(i, way, step + 1, order).start()
+                        for later in after[step]:
+                            if later < steps_of(way, order):
+                                ring_copy(i, way, later, order).start()
         if share:
             for i in range(count):
                 pair_copy(i, -step - 1 if step < 3 else 4).start()

time: 116 us -> 112 us (0.966)
  Pallas kernels: 93.3 us -> 88.7 us
    pallas_call x2, Pallas kernels: 75 us -> 72.3 us  [gather_blocks(): pl.pallas_call(functools.partial(gather_kernel, count, share, near), out_...]
    pallas_call x1, Pallas kernels: 12.2 us -> 10.4 us  [exchange(): pl.pallas_call(exchange_kernel, out_shape=jax.ShapeDtypeStruct(windows.sh...]
where the time goes in v8:
time: 112 us; the launch traced here: 111 us
  Pallas kernels  88.7 us (79%)
  other arithmetic  8.74 us (8%)
  matrix products  8.7 us (8%)
  local copies, waits for them, and re-layouts  4.66 us (4%)
    pallas_call x2, Pallas kernels, gather_blocks(): pl.pallas_call(functools.partial(gather_kernel, count, share, near), out_...  72.3 us
    pallas_call x1, Pallas kernels, exchange(): pl.pallas_call(exchange_kernel, out_shape=jax.ShapeDtypeStruct(windows.sh...  10.4 us
    pallas_call x1, Pallas kernels, vocoder(): pl.pallas_call(functools.partial(vocoder_kernel, groups, piece), out_shap...  6.11 us
    dot_general x1, matrix products, shards(): conv_out = jnp.dot(filters, outward, preferred_element_type=jnp.float32)  4.36 us
    dot_general x1, matrix products, shards(): jnp.dot(hit.astype(BF), portion, preferred_element_type=jnp.float32)  3.07 us
    select_n x3, other arithmetic, shards(): pick = lambda both: jnp.where(core == 0, both[0], both[1])  2.4 us

profile of v8, /device:TPU:1, one launch (start us, length us, event | category | flops | bytes accessed | tf_op | source)
XLA Modules:
  0.0 111.1 jit_solution(9305466050906413304)
XLA Ops:
  0.0 1.0 slice_select_fusion
  1.0 0.1 select_n.124
  1.1 0.0 copy-start.5
  1.1 0.0 copy-start.4
  1.1 0.2 convolution_convert_fusion
  1.3 0.1 reshape.177
  1.4 0.8 slice_select_fusion.2
  2.2 0.6 fusion.38.refs_0_
  2.8 0.9 reshape.178
  3.7 0.0 copy-start.6
  3.7 0.6 fusion.40.refs_1_
  4.3 53.1 %gather1.1 = (bf16[2,8,8,8,2688]{4,3,2,1,0:T(8,128)(2,1)}, bf16[2,8,8,8,2048]{4,3,2,1,0:T(8,128)(2,1)}, s32[2,1,64]{2,1,0:T(1,128)}) custom-call(bf16[8,2688]{1,0:T(8,128)(2,1)} %fusion.38.refs_0_, bf16[8,2048]{1,0:T(8,128)(2,1)} %fusion.40.refs_1_, s32[1,64]{1,0:T(1,128)} %refs_2_.1), custom_call_target="tpu_custom_call" | custom-call | tf_op jit(solution)/shard_map/gather1/pallas_call | solution.py:193
  57.5 0.7 slice_bitcast_fusion
  58.2 0.8 pad_add_fusion.1
  59.0 0.7 copy.26
  59.7 0.1 reduce-window.18
  59.8 0.1 fusion.39
  59.9 0.1 convert_reduce_fusion
  60.0 0.1 compare_select_fusion.6
  60.1 0.1 fusion.27
  60.2 0.1 fusion.28
  60.3 0.1 fusion.29
  60.4 0.1 fusion.30
  60.5 0.7 fusion.25
  61.2 0.1 compare_select_fusion.2
  61.3 0.1 fusion.31
  61.4 0.1 fusion.32
  61.5 0.1 fusion.33
  61.6 0.1 fusion.34
  61.7 0.9 fusion.26
  62.5 4.4 %fusion.47 = (f32[64]{0:T(128)S(1)}, f32[64,384]{1,0:T(8,128)S(1)}) fusion(f32[64,384]{1,0:T(8,128)S(1)} %fusion.26, bf16[1024,2688]{1,0:T(8,128)(2,1)} %bitcast.54, pred[64,2304]{1,0:T(8,128)(4,1)S(1)} %fusion.34), kind=kOutput, calls=%fused_computation.101 | convolution fusion | flops 352501696 | bytes 5849344 | tf_op jit(solution)/shard_map/dot_general | solution.py:331
  66.9 0.2 multiply_reduce_fusion
  67.1 0.0 copy-done.3
  67.1 0.2 convolution_convert_fusion.1
  67.3 0.7 select_add_fusion.refs_0_
  68.0 19.1 %gather2.1 = bf16[1,8,8,64,128]{4,3,2,1,0:T(8,128)(2,1)} custom-call(bf16[64,128]{1,0:T(8,128)(2,1)} %select_add_fusion.refs_0_), custom_call_target="tpu_custom_call" | custom-call | tf_op jit(solution)/shard_map/gather2/pallas_call | solution.py:193
  87.2 0.3 reduce-window.11
  87.5 0.1 slice.136
  87.6 0.1 reduce-window.14
  87.6 0.1 slice_reduce_fusion
  87.7 0.1 add_bitcast_fusion
  87.8 0.8 gather_fusion
  88.6 0.1 fusion.44
  88.7 0.1 select_reduce_fusion.2
  88.8 0.2 select_reduce_fusion.1
  89.0 0.1 fusion.43
  89.1 0.3 select_reduce_fusion
  89.3 0.1 reduce_sum.69
  89.4 0.1 reshape.172
  89.5 0.1 copy.24
  89.6 0.1 copy.25
  89.7 0.1 reshape.171
  89.7 0.5 broadcast.184
  90.2 0.7 reduce.10
  90.9 0.1 squeeze.6
  91.0 0.1 fusion.46
  91.1 0.1 ge.26
  91.2 0.1 lt.60
  91.3 0.1 select_reduce_fusion.3
  91.4 0.1 iota_add_fusion
  91.5 0.1 add.134
  91.5 3.1 %fusion.15 = bf16[320,128]{1,0:T(8,128)(2,1)} fusion(bf16[4096,128]{1,0:T(8,128)(2,1)} %bitcast.42, s32[4096]{0:T(1024)S(1)} %lt.60, s32[4096]{0:T(1024)S(1)} %ge.26, s32[320]{0:T(512)S(1)} %add.134), kind=kOutput, calls=%fused_computation.12 | convolution fusion | flops 339517440 | bytes 1164544 | tf_op jit(solution)/shard_map/dot_general | solution.py:362
  94.6 10.4 %exchange.1 = bf16[8,40,128]{2,1,0:T(8,128)(2,1)} custom-call(bf16[8,40,128]{2,1,0:T(8,128)(2,1)} %bitcast.46), custom_call_target="tpu_custom_call" | custom-call | tf_op jit(solution)/shard_map/exchange/pallas_call | solution.py:236
  105.0 6.1 %vocoder.1 = bf16[256,8,256]{2,1,0:T(8,128)(2,1)} custom-call(bf16[320,128]{1,0:T(8,128)(2,1)} %bitcast.43, bf16[7,80,512]{2,1,0:T(8,128)(2,1)} %pre.1, bf16[2,512,2048]{2,1,0:T(8,128)(2,1)} %bitcast.41), custom_call_target="tpu_custom_call" | custom-call | tf_op jit(solution)/shard_map/vocoder/pallas_call | solution.py:433
  (22 shorter events, 0.1 us)
Async XLA Ops:
  0.0 1.1 copy-start
  0.0 67.1 %copy-start.3 = (f32[384]{0:T(512)S(1)}, f32[384]{0:T(512)}, u32[]{:S(2)}) copy-start(f32[384]{0:T(512)} %param.20) | copy-start | bytes 4612
  0.0 67.1 %copy-start.2 = (bf16[384,80]{0,1:T(8,128)(2,1)S(1)}, bf16[384,80]{0,1:T(8,128)(2,1)}, u32[]{:S(2)}) copy-start(bf16[384,80]{0,1:T(8,128)(2,1)} %param.21) | copy-start | bytes 184324
  0.0 87.2 %copy-start.1 = (s32[1,4096]{1,0:T(1,128)S(1)}, s32[1,4096]{1,0:T(1,128)}, u32[]{:S(2)}) copy-start(s32[1,4096]{1,0:T(1,128)} %param.13) | copy-start | bytes 49156
  1.1 87.6 %copy-start.5 = (s32[1,64]{1,0:T(1,128)S(1)}, s32[1,64]{1,0:T(1,128)}, u32[]{:S(2)}) copy-start(s32[1,64]{1,0:T(1,128)} %param.15) | copy-start | bytes 772
  1.1 87.9 %copy-start.4 = (s32[1,64]{1,0:T(1,128)S(1)}, s32[1,64]{1,0:T(1,128)}, u32[]{:S(2)}) copy-start(s32[1,64]{1,0:T(1,128)} %param.14) | copy-start | bytes 772
  3.7 87.6 %copy-start.6 = (s32[1,1,8]{2,1,0:T(1,128)S(1)}, s32[1,1,8]{2,1,0:T(1,128)}, u32[]{:S(2)}) copy-start(s32[1,1,8]{2,1,0:T(1,128)} %param.16) | copy-start | bytes 100

commit v9 on v8

--- a/solution.py
+++ b/solution.py
@@ -131,14 +131,14 @@
             if order > 0:
                 first_copy(i, order).wait_recv()
             for way in range(2):
-                for step in (0, 1) if leap else (0,):
+                for step in (1, 0) if leap else (0,):
                     ring_copy(i, way, step, order).start()
     for copy in own:
         copy.wait()
     if share:
         for i in range(count):
             pair_copy(i, 0).start()
-    after = {0: (), 1: (2, 3), 2: (), 3: ()} if leap else {0: (1,), 1: (2,), 2: (3,), 3: ()}
+    after = {0: (), 1: (3, 2), 2: (), 3: ()} if leap else {0: (1,), 1: (2,), 2: (3,), 3: ()}
     for step in (1, 0, 2, 3) if leap else (0, 1, 2, 3):
         for order in ORDER:
             for i in range(count):

time: 112 us -> 111 us (level)
  no operation moved by 1% of the time
where the time goes in v9:
time: 111 us
  Pallas kernels  88.3 us (80%)
  other arithmetic  8.74 us (8%)
  matrix products  8.7 us (8%)
  local copies, waits for them, and re-layouts  4.66 us (4%)
    pallas_call x2, Pallas kernels, gather_blocks(): pl.pallas_call(functools.partial(gather_kernel, count, share, near), out_...  72.1 us
    pallas_call x1, Pallas kernels, exchange(): pl.pallas_call(exchange_kernel, out_shape=jax.ShapeDtypeStruct(windows.sh...  10.1 us
    pallas_call x1, Pallas kernels, vocoder(): pl.pallas_call(functools.partial(vocoder_kernel, groups, piece), out_shap...  6.12 us
    dot_general x1, matrix products, shards(): conv_out = jnp.dot(filters, outward, preferred_element_type=jnp.float32)  4.36 us
    dot_general x1, matrix products, shards(): jnp.dot(hit.astype(BF), portion, preferred_element_type=jnp.float32)  3.07 us
    select_n x3, other arithmetic, shards(): pick = lambda both: jnp.where(core == 0, both[0], both[1])  2.4 us

profile of v9, /device:TPU:1, one launch (start us, length us, event | category | flops | bytes accessed | tf_op | source)
XLA Modules:
  0.0 110.7 jit_solution(8411853686220678934)
XLA Ops:
  0.0 1.0 slice_select_fusion
  1.0 0.1 select_n.124
  1.1 0.0 copy-start.5
  1.1 0.0 copy-start.4
  1.1 0.2 convolution_convert_fusion
  1.3 0.1 reshape.177
  1.4 0.8 slice_select_fusion.2
  2.2 0.6 fusion.38.refs_0_
  2.8 0.9 reshape.178
  3.7 0.0 copy-start.6
  3.7 0.6 fusion.40.refs_1_
  4.3 53.1 %gather1.1 = (bf16[2,8,8,8,2688]{4,3,2,1,0:T(8,128)(2,1)}, bf16[2,8,8,8,2048]{4,3,2,1,0:T(8,128)(2,1)}, s32[2,1,64]{2,1,0:T(1,128)}) custom-call(bf16[8,2688]{1,0:T(8,128)(2,1)} %fusion.38.refs_0_, bf16[8,2048]{1,0:T(8,128)(2,1)} %fusion.40.refs_1_, s32[1,64]{1,0:T(1,128)} %refs_2_.1), custom_call_target="tpu_custom_call" | custom-call | tf_op jit(solution)/shard_map/gather1/pallas_call | solution.py:193
  57.5 0.7 slice_bitcast_fusion
  58.2 0.8 pad_add_fusion.1
  59.0 0.7 copy.26
  59.7 0.1 reduce-window.18
  59.8 0.1 fusion.39
  59.9 0.1 convert_reduce_fusion
  60.0 0.1 compare_select_fusion.6
  60.1 0.1 fusion.27
  60.2 0.1 fusion.28
  60.3 0.1 fusion.29
  60.4 0.1 fusion.30
  60.5 0.7 fusion.25
  61.2 0.1 compare_select_fusion.2
  61.3 0.1 fusion.31
  61.4 0.1 fusion.32
  61.5 0.1 fusion.33
  61.6 0.1 fusion.34
  61.7 0.9 fusion.26
  62.5 4.4 %fusion.47 = (f32[64]{0:T(128)S(1)}, f32[64,384]{1,0:T(8,128)S(1)}) fusion(f32[64,384]{1,0:T(8,128)S(1)} %fusion.26, bf16[1024,2688]{1,0:T(8,128)(2,1)} %bitcast.54, pred[64,2304]{1,0:T(8,128)(4,1)S(1)} %fusion.34), kind=kOutput, calls=%fused_computation.101 | convolution fusion | flops 352501696 | bytes 5849344 | tf_op jit(solution)/shard_map/dot_general | solution.py:331
  66.9 0.2 multiply_reduce_fusion
  67.1 0.2 convolution_convert_fusion.1
  67.3 0.7 select_add_fusion.refs_0_
  68.0 19.0 %gather2.1 = bf16[1,8,8,64,128]{4,3,2,1,0:T(8,128)(2,1)} custom-call(bf16[64,128]{1,0:T(8,128)(2,1)} %select_add_fusion.refs_0_), custom_call_target="tpu_custom_call" | custom-call | tf_op jit(solution)/shard_map/gather2/pallas_call | solution.py:193
  87.0 0.3 reduce-window.11
  87.3 0.1 slice.136
  87.4 0.1 reduce-window.14
  87.4 0.1 slice_reduce_fusion
  87.5 0.1 add_bitcast_fusion
  87.6 0.8 gather_fusion
  88.4 0.1 fusion.44
  88.5 0.1 select_reduce_fusion.2
  88.6 0.2 select_reduce_fusion.1
  88.8 0.1 fusion.43
  88.9 0.3 select_reduce_fusion
  89.2 0.1 reduce_sum.69
  89.2 0.1 reshape.172
  89.3 0.1 copy.24
  89.4 0.1 copy.25
  89.5 0.1 reshape.171
  89.6 0.5 broadcast.184
  90.1 0.7 reduce.10
  90.8 0.1 squeeze.6
  90.8 0.1 fusion.46
  90.9 0.1 ge.26
  91.0 0.1 lt.60
  91.1 0.0 copy-done.6
  91.1 0.1 select_reduce_fusion.3
  91.2 0.1 iota_add_fusion
  91.3 0.1 add.134
  91.4 3.1 %fusion.15 = bf16[320,128]{1,0:T(8,128)(2,1)} fusion(bf16[4096,128]{1,0:T(8,128)(2,1)} %bitcast.42, s32[4096]{0:T(1024)S(1)} %lt.60, s32[4096]{0:T(1024)S(1)} %ge.26, s32[320]{0:T(512)S(1)} %add.134), kind=kOutput, calls=%fused_computation.12 | convolution fusion | flops 339517440 | bytes 1164544 | tf_op jit(solution)/shard_map/dot_general | solution.py:362
  94.4 10.1 %exchange.1 = bf16[8,40,128]{2,1,0:T(8,128)(2,1)} custom-call(bf16[8,40,128]{2,1,0:T(8,128)(2,1)} %bitcast.46), custom_call_target="tpu_custom_call" | custom-call | tf_op jit(solution)/shard_map/exchange/pallas_call | solution.py:236
  104.5 6.1 %vocoder.1 = bf16[256,8,256]{2,1,0:T(8,128)(2,1)} custom-call(bf16[320,128]{1,0:T(8,128)(2,1)} %bitcast.43, bf16[7,80,512]{2,1,0:T(8,128)(2,1)} %pre.1, bf16[2,512,2048]{2,1,0:T(8,128)(2,1)} %bitcast.41), custom_call_target="tpu_custom_call" | custom-call | tf_op jit(solution)/shard_map/vocoder/pallas_call | solution.py:433
  (22 shorter events, 0.1 us)
Async XLA Ops:
  0.0 1.1 %copy-start = (bf16[256,384]{1,0:T(8,128)(2,1)S(1)}, bf16[256,384]{1,0:T(8,128)(2,1)}, u32[]{:S(2)}) copy-start(bf16[256,384]{1,0:T(8,128)(2,1)} %param.17) | copy-start | bytes 589828
  0.0 67.1 %copy-start.3 = (f32[384]{0:T(512)S(1)}, f32[384]{0:T(512)}, u32[]{:S(2)}) copy-start(f32[384]{0:T(512)} %param.20) | copy-start | bytes 4612
  0.0 67.1 %copy-start.2 = (bf16[384,80]{0,1:T(8,128)(2,1)S(1)}, bf16[384,80]{0,1:T(8,128)(2,1)}, u32[]{:S(2)}) copy-start(bf16[384,80]{0,1:T(8,128)(2,1)} %param.21) | copy-start | bytes 184324
  0.0 87.0 %copy-start.1 = (s32[1,4096]{1,0:T(1,128)S(1)}, s32[1,4096]{1,0:T(1,128)}, u32[]{:S(2)}) copy-start(s32[1,4096]{1,0:T(1,128)} %param.13) | copy-start | bytes 49156
  1.1 87.4 %copy-start.5 = (s32[1,64]{1,0:T(1,128)S(1)}, s32[1,64]{1,0:T(1,128)}, u32[]{:S(2)}) copy-start(s32[1,64]{1,0:T(1,128)} %param.15) | copy-start | bytes 772
  1.1 87.7 %copy-start.4 = (s32[1,64]{1,0:T(1,128)S(1)}, s32[1,64]{1,0:T(1,128)}, u32[]{:S(2)}) copy-start(s32[1,64]{1,0:T(1,128)} %param.14) | copy-start | bytes 772
  3.7 87.4 %copy-start.6 = (s32[1,1,8]{2,1,0:T(1,128)S(1)}, s32[1,1,8]{2,1,0:T(1,128)}, u32[]{:S(2)}) copy-start(s32[1,1,8]{2,1,0:T(1,128)} %param.16) | copy-start | bytes 100
